TPU v7x, 1024 devices: a whole 4x8x16 slice. The times are simulated.
1024 devices in a mesh: lat: 128 (over x, y, z_lo), lev: 8 (over z_hi, core).
Axes of the slice: x: 4, y: 8, z: 16 (z_hi: 4, z_lo: 4; z = z_hi * 4 + z_lo), core: 2. Of those that a mesh axis runs over, the one named last changes fastest.
Arguments:
- fields: float32 [3, 64, 256, 1024], P(None, 'lev', 'lat'), may hold values from -6 to 6
- north_courant: float32 [64, 256, 1024], P('lev', 'lat'), may hold values from 0.05 to 0.3
- south_courant: float32 [64, 256, 1024], P('lev', 'lat'), may hold values from 0.05 to 0.3
- east_courant: float32 [64, 256, 1024], P('lev', 'lat'), may hold values from 0.05 to 0.3
- limiter: int32 [64, 256, 1024], P('lev', 'lat'), may hold values from 0 to 3
- thickness: float32 [64, 256, 1024], P('lev', 'lat'), may hold values from 0.5 to 2
- sunlit: int32 [256, 8], P('lat', 'lev'), may hold values from 0 to 1, as said below
- absorb: float32 [2, 64], replicated, may hold values from 0.002 to 0.05
- solar_flux: float32 [64], replicated, may hold values from 0.1 to 1
Outputs:
- column_fields: float32 [3, 64, 256, 1024], P(None, None, 'lat', 'lev')
Inputs may be any that keep to these rules, and one draw needn't show every extreme that they name: sunlit[r, b] + sunlit[(r + 128) mod 256, b] = 1 for every row r and block b: of two rows half the grid apart, exactly one is lit.
All inputs are finite; a program needn't handle non-finite values.
Results may differ from a plain program's by a relative error of at most 0.00019.
Values sent between devices are 32-bit elements; how exact they have to be, the bound alone decides.
No kernel may reach another device: no remote copies, remote signals or barrier semaphores. Data moves between devices by JAX's collectives and lax.ppermute only.
A program may use at most 32 MiB of HBM per device.

v0:
```python
from functools import partial

import jax
import jax.numpy as jnp
from jax import lax
from jax.sharding import PartitionSpec as P

lw_rate = 0.2
lw_damp = 0.1


def passed_along(x, axis, by):
    size = lax.axis_size(axis)
    pairs = [(i, i + by) for i in range(size) if 0 <= i + by < size]
    return lax.ppermute(x, axis, pairs)


def pick_slope(limiter_code, back_diff, fore_diff):
    centred = 0.5 * (back_diff + fore_diff)
    return jnp.where(
        limiter_code == 1,
        back_diff,
        jnp.where(
            limiter_code == 2,
            fore_diff,
            jnp.where(limiter_code == 3, centred, jnp.zeros_like(centred)),
        ),
    )


def face_fluxes(values, limiter_code, back_diff, fore_diff, northward, southward):
    slopes = pick_slope(limiter_code, back_diff, fore_diff)
    rising = northward * (values + 0.5 * (1.0 - northward) * slopes)
    sinking = southward * (values - 0.5 * (1.0 - southward) * slopes)
    return (rising, sinking)


def zonal_flux(fields, eastward, limiter):
    back_diff = fields - jnp.roll(fields, 1, axis=3)
    fore_diff = jnp.roll(fields, -1, axis=3) - fields
    slopes = pick_slope(limiter[None], back_diff, fore_diff)
    outgoing = eastward[None] * (fields + 0.5 * (1.0 - eastward[None]) * slopes)
    return (outgoing, jnp.roll(outgoing, 1, axis=3))


def combine(fields, rising, sinking, from_below, from_above, outgoing, incoming):
    return fields - (rising + sinking) + (from_below + from_above) - (outgoing - incoming)


def regrid_column(layer_fields, layer_depth):
    levels = layer_depth.shape[0]
    top_edge = jnp.cumsum(layer_depth, axis=0)
    low_edge = top_edge - layer_depth
    target = top_edge[-1] / levels
    level_index = jnp.arange(levels, dtype=jnp.float32)[:, None]
    target_low = level_index * target[None]
    target_high = (level_index + 1.0) * target[None]
    intersection = jnp.maximum(
        jnp.minimum(top_edge[None], target_high[:, None])
        - jnp.maximum(low_edge[None], target_low[:, None]),
        0.0,
    )
    shifted = jnp.einsum(
        "kjc,fjc->fkc", intersection, layer_fields, precision=lax.Precision.HIGHEST
    )
    return (shifted / target[None, None], target)


def regrid_item(column_slab):
    return regrid_column(column_slab[:3], column_slab[3])


def regrid(exchanged):
    regridded, depths = lax.map(regrid_item, jnp.moveaxis(exchanged, 2, 0))
    return (jnp.moveaxis(regridded, 0, 2), depths[None, None])


def shortwave(packet, absorb, solar_flux):
    levels = (packet.shape[0] - 1) // 2
    vapour = packet[:levels]
    ozone_mix = packet[levels : 2 * levels]
    layer_depth = packet[2 * levels]
    opacity = (
        absorb[0][:, None, None] * (vapour * vapour)[None]
        + absorb[1][:, None, None] * (ozone_mix * ozone_mix)[None]
    )
    optical = opacity * layer_depth[None, None]
    counter = jnp.arange(levels)
    triangle = (counter[:, None] > counter[None, :]).astype(jnp.float32)
    overhead = jnp.einsum("km,bmc->bkc", triangle, optical, precision=lax.Precision.HIGHEST)
    incoming = solar_flux[:, None, None] * jnp.exp(-overhead)
    absorbed = jnp.sum(incoming * (1.0 - jnp.exp(-optical)), axis=0)
    return absorbed / layer_depth[None]


def shortwave_rows(packet, absorb, solar_flux):
    heated = lax.map(
        partial(shortwave, absorb=absorb, solar_flux=solar_flux), jnp.moveaxis(packet, 1, 0)
    )
    return jnp.moveaxis(heated, 0, 1)


def longwave(temper):
    beneath = jnp.concatenate([jnp.zeros_like(temper[:1]), temper[:-1]], 0)
    overlying = jnp.concatenate([temper[1:], jnp.zeros_like(temper[:1])], 0)
    return lw_rate * (beneath + overlying - 2.0 * temper) - lw_damp * temper


def local(
    fields,
    north_courant,
    south_courant,
    east_courant,
    limiter,
    thickness,
    sunlit,
    absorb,
    solar_flux,
):
    outgoing, incoming = zonal_flux(fields, east_courant, limiter)
    limit_float = limiter.astype(jnp.float32)
    top_pack = jnp.concatenate(
        [
            fields[:, :, -2:-1],
            fields[:, :, -1:],
            north_courant[None, :, -1:],
            limit_float[None, :, -1:],
        ],
        0,
    )
    bottom_pack = jnp.concatenate(
        [fields[:, :, :1], fields[:, :, 1:2], south_courant[None, :, :1], limit_float[None, :, :1]],
        0,
    )
    below = passed_along(top_pack, "lat", 1)
    above = passed_along(bottom_pack, "lat", -1)
    lower_fields = jnp.concatenate([below[0:3], below[3:6]], 2)
    upper_fields = jnp.concatenate([above[0:3], above[3:6]], 2)
    extended = jnp.concatenate([lower_fields, fields, upper_fields], 2)
    values = extended[:, :, 1:-1]
    back_diff = values - extended[:, :, :-2]
    fore_diff = extended[:, :, 2:] - values
    own_rise, own_sink = face_fluxes(
        fields,
        limiter[None],
        back_diff[:, :, 1:-1],
        fore_diff[:, :, 1:-1],
        north_courant[None],
        south_courant[None],
    )
    low_slope = pick_slope(below[7:8], back_diff[:, :, :1], fore_diff[:, :, :1])
    low_courant = below[6:7]
    lowest = low_courant * (values[:, :, :1] + 0.5 * (1.0 - low_courant) * low_slope)
    high_slope = pick_slope(above[7:8], back_diff[:, :, -1:], fore_diff[:, :, -1:])
    high_courant = above[6:7]
    highest = high_courant * (values[:, :, -1:] - 0.5 * (1.0 - high_courant) * high_slope)
    from_below = jnp.concatenate([lowest, own_rise[:, :, :-1]], 2)
    from_above = jnp.concatenate([own_sink[:, :, 1:], highest], 2)
    advected = combine(fields, own_rise, own_sink, from_below, from_above, outgoing, incoming)
    packed = jnp.concatenate([advected, thickness[None]], 0)
    remapped, depths = regrid(
        lax.all_to_all(packed, "lev", split_axis=3, concat_axis=1, tiled=True)
    )
    layer_depth = depths[0, 0]
    packet = jnp.concatenate([remapped[1], remapped[2], layer_depth[None]], 0)
    lit_rows = sunlit[:, 0].astype(jnp.float32)
    cooling = longwave(remapped[0])
    solar_heat = shortwave_rows(packet, absorb, solar_flux) * lit_rows[None, :, None]
    heating = solar_heat + cooling
    warmed = remapped[0] + heating
    return jnp.concatenate([warmed[None], remapped[1:]], 0)


def solution(mesh):
    in_specs = (
        P(None, "lev", "lat", None),
        P("lev", "lat", None),
        P("lev", "lat", None),
        P("lev", "lat", None),
        P("lev", "lat", None),
        P("lev", "lat", None),
        P("lat", "lev"),
        P(),
        P(),
    )
    out_specs = P(None, None, "lat", "lev")
    return jax.shard_map(local, mesh=mesh, in_specs=in_specs, out_specs=out_specs, check_vma=False)
```

profile of v0, /device:TPU:6, one launch (start us, length us, event | category | flops | bytes accessed | tf_op | source)
XLA Modules:
  0.0 116.4 jit_solution(10697716040998350106)
XLA Ops:
  0.0 1.0 copy.146
  1.1 0.0 copy-start.5
  1.1 0.9 copy.136
  2.0 0.9 copy_convert_fusion
  2.8 0.9 copy.129
  3.8 4.3 %collective-permute-start = (f32[8,8,1,1024]{3,1,2,0:T(8,128)S(1)}, f32[8,8,1,1024]{3,1,2,0:T(8,128)S(1)}, u32[]{:S(2)}, u32[]{:S(2)}) collective-permute-start(f32[8,8,1,1024]{3,1,2,0:T(8,128)S(1)} %get-tuple-element.149), channel_id=1, source_target_pairs={{0,8},{8,16},{16,24},{24,32},{32,40},{40,48},{48,56},{56,64},{64,7... | collective-permute-start | bytes 786440 | tf_op jit(solution)/shard_map/ppermute | solution.py:15
  8.1 8.8 %collective-permute-start.1 = (f32[8,8,1,1024]{3,1,2,0:T(8,128)S(1)}, f32[8,8,1,1024]{3,1,2,0:T(8,128)S(1)}, u32[]{:S(2)}, u32[]{:S(2)}) collective-permute-start(f32[8,8,1,1024]{3,1,2,0:T(8,128)S(1)} %get-tuple-element.150), channel_id=1, source_target_pairs={{8,0},{16,8},{24,16},{32,24},{40,32},{48,40},{56,48},{64,56},{72,6... | collective-permute-start | bytes 786440 | tf_op jit(solution)/shard_map/ppermute | solution.py:15
  16.9 0.1 fusion.39
  17.1 0.1 broadcast_compare_fusion.2
  17.3 0.1 fusion.38
  17.6 4.4 %collective-permute-done = f32[8,8,1,1024]{3,1,2,0:T(8,128)S(1)} collective-permute-done((f32[8,8,1,1024]{3,1,2,0:T(8,128)S(1)}, f32[8,8,1,1024]{3,1,2,0:T(8,128)S(1)}, u32[]{:S(2)}, u32[]{:S(2)}) %collective-permute-start) | collective-permute-done | bytes 262176 | tf_op jit(solution)/shard_map/ppermute | solution.py:15
  22.1 1.5 %collective-permute-done.1 = f32[8,8,1,1024]{3,1,2,0:T(8,128)S(1)} collective-permute-done((f32[8,8,1,1024]{3,1,2,0:T(8,128)S(1)}, f32[8,8,1,1024]{3,1,2,0:T(8,128)S(1)}, u32[]{:S(2)}, u32[]{:S(2)}) %collective-permute-start.1) | collective-permute-done | bytes 262176 | tf_op jit(solution)/shard_map/ppermute | solution.py:15
  23.6 0.1 maximum_subtract_fusion
  23.7 0.2 subtract_multiply_fusion
  24.0 0.1 slice.219
  24.1 0.1 subtract_multiply_fusion.1
  24.2 0.1 fusion.33
  24.4 4.3 %copy.157 = f32[4,8,2,1024]{1,2,0,3:T(2,128)} copy(f32[4,8,2,1024]{3,1,2,0:T(8,128)S(1)} %pad_maximum_fusion.4) | data formatting | bytes 524288 | tf_op jit(solution)/shard_map/concatenate | solution.py:160
  28.7 8.9 %reshape.151 = f32[8,1,8192]{2,1,0:T(1,128)} reshape(f32[1024,4,2,8]{3,2,1,0:T(2,128)} %bitcast.116) | data formatting | bytes 524288
  37.6 17.3 %all-to-all-start = ((f32[8,1,8192]{2,1,0:T(1,128)}), f32[8,1,8192]{2,1,0:T(1,128)S(1)}, u32[]{:S(2)}, u32[]{:S(2)}) async-start(f32[8,1,8192]{2,1,0:T(1,128)} %reshape.151), calls=%async_computation | async-start | bytes 524288 | tf_op jit(solution)/shard_map/all_to_all | solution.py:162
  54.9 21.3 %all-to-all-done = f32[8,1,8192]{2,1,0:T(1,128)S(1)} async-done(((f32[8,1,8192]{2,1,0:T(1,128)}), f32[8,1,8192]{2,1,0:T(1,128)S(1)}, u32[]{:S(2)}, u32[]{:S(2)}) %all-to-all-start) | async-done | bytes 262176 | tf_op jit(solution)/shard_map/all_to_all | solution.py:162
  76.3 0.6 broadcast.206
  76.8 1.3 %reduce = f32[8,8192]{1,0:T(8,128)S(1)} reduce(f32[8,1,8192]{2,1,0:T(1,128)S(1)} %all-to-all-done, f32[]{:T(128)} %broadcast.206), dimensions={1}, to_apply=%all_to_all.13.reduce_sub_computation | reduce | bytes 524292 | tf_op jit(solution)/shard_map/all_to_all | solution.py:162
  78.1 8.3 %reshape.152 = f32[1024,4,2,8]{3,2,1,0:T(2,128)} reshape(f32[8,8192]{1,0:T(8,128)S(1)} %reduce) | data formatting | bytes 524288
  86.4 5.1 %copy.164 = f32[4,8,2,8,128]{4,1,3,2,0:T(8,128)S(1)} copy(f32[4,8,2,8,128]{1,2,0,4,3:T(2,128)} %bitcast.117) | data formatting | bytes 524288 | tf_op jit(solution)/shard_map/all_to_all | solution.py:162
  91.6 0.0 copy-start.6
  91.6 18.5 %while.22 = (s32[]{:T(128)}, f32[2,3,64,128]{3,2,0,1:T(8,128)S(1)}, f32[2,128]{1,0:T(2,128)S(1)}, f32[2,4,64,128]{3,2,0,1:T(8,128)S(1)}, s32[]{:T(128)}, /*index=5*/s32[]{:T(128)}, s32[]{}, f32[]{:T(128)}) while((s32[]{:T(128)}, f32[2,3,64,128]{3,2,0,1:T(8,128)S(1)}, f32[2,128]{1,0:T(2,128)S(1)}, f32[2,4,64,128]{3,2,0,1:T(8,128)S(1)}, ...), condition=%wide.region_2.3_spmd, body=%wide.region_0.2_spmd.sunk | while | flops 21536964 | bytes 1609849 | solution.py:74
  91.6 0.1 copy.184
  91.7 0.1 copy.185
  91.8 0.1 reduce_window_sum.12
  91.9 0.1 copy.186
  92.0 0.1 broadcast_multiply_fusion.2
  92.2 0.1 copy.187
  92.3 8.3 %fusion.51 = f32[1,3,64,128]{2,1,3,0:T(4,128)S(1)} fusion(f32[64,128]{0,1:T(8,128)S(1)} %get-tuple-element.219, f32[64,128]{0,1:T(8,128)S(1)} %sub.115, f32[64,128]{0,1:T(8,128)S(1)} %get-tuple-element.220, f32[64,128]{0,1:T(8,128)S(1)} %copy.186, f32[1,3,64,128]{2,1,3,0:T(4,128)S(1)} %copy.187, f32[128]{0:T(128)S(1)} %get-tuple-element.218), kind=kOutput, calls=%fused_computation.11.clone.1 | convolution fusion | flops 20996096 | bytes 328192 | tf_op jit(solution)/shard_map/while/body/eval_jaxpr/kjc,fjc->fkc/dot_general | solution.py:63
  100.6 0.1 copy.188
  100.9 0.1 copy.184
  101.0 0.1 copy.185
  101.0 0.1 reduce_window_sum.12
  101.1 0.1 copy.186
  101.3 0.1 broadcast_multiply_fusion.2
  101.4 0.1 copy.187
  101.5 8.3 %fusion.51 = f32[1,3,64,128]{2,1,3,0:T(4,128)S(1)} fusion(f32[64,128]{0,1:T(8,128)S(1)} %get-tuple-element.219, f32[64,128]{0,1:T(8,128)S(1)} %sub.115, f32[64,128]{0,1:T(8,128)S(1)} %get-tuple-element.220, f32[64,128]{0,1:T(8,128)S(1)} %copy.186, f32[1,3,64,128]{2,1,3,0:T(4,128)S(1)} %copy.187, f32[128]{0:T(128)S(1)} %get-tuple-element.218), kind=kOutput, calls=%fused_computation.11.clone.1 | convolution fusion | flops 20996096 | bytes 328192 | tf_op jit(solution)/shard_map/while/body/eval_jaxpr/kjc,fjc->fkc/dot_general | solution.py:63
  109.9 0.1 copy.188
  110.2 5.3 %while.23 = (s32[]{:T(128)}, f32[2,64,128]{2,1,0:T(8,128)S(1)}, f32[64]{0:T(128)S(1)}, f32[2,64]{1,0:T(2,128)S(1)}, f32[2,129,128]{2,1,0:T(8,128)S(1)}, /*index=5*/s32[]{:T(128)}, s32[]{:T(128)}, s32[]{}, s32[]{}) while((s32[]{:T(128)}, f32[2,64,128]{2,1,0:T(8,128)S(1)}, f32[64]{0:T(128)S(1)}, f32[2,64]{1,0:T(2,128)S(1)}, ...), condition=%wide.region_5.6_spmd, body=%wide.region_3.5_spmd.sunk | while | flops 410013696 | bytes 298889 | solution.py:97
  110.2 2.5 %fusion.55 = f32[64,128]{1,0:T(8,128)S(1)} fusion(f32[128]{0:T(128)S(1)} %fusion.53, f32[64,128]{1,0:T(8,128)S(1)} %get-tuple-element.227, f32[64]{0:T(128)S(1)} %get-tuple-element.228, f32[64,128]{1,0:T(8,128)S(1)} %get-tuple-element.229, f32[64]{0:T(128)S(1)} %get-tuple-element.230, f32[64]{0:T(128)S(1)} %get-tuple-element.275), kind=kOutput, calls=%fused_computation.23.clone.1 | convolution fusion | flops 409989120 | bytes 99584 | tf_op jit(solution)/shard_map/while/body/eval_jaxpr/km,bmc->bkc/dot_general | solution.py:90
  112.9 2.5 %fusion.55 = f32[64,128]{1,0:T(8,128)S(1)} fusion(f32[128]{0:T(128)S(1)} %fusion.53, f32[64,128]{1,0:T(8,128)S(1)} %get-tuple-element.227, f32[64]{0:T(128)S(1)} %get-tuple-element.228, f32[64,128]{1,0:T(8,128)S(1)} %get-tuple-element.229, f32[64]{0:T(128)S(1)} %get-tuple-element.230, f32[64]{0:T(128)S(1)} %get-tuple-element.275), kind=kOutput, calls=%fused_computation.23.clone.1 | convolution fusion | flops 409989120 | bytes 99584 | tf_op jit(solution)/shard_map/while/body/eval_jaxpr/km,bmc->bkc/dot_general | solution.py:90
  115.4 0.1 fusion.35
  115.6 0.8 copy.162
  (71 shorter events, 0.9 us)
Async XLA Ops:
  0.0 17.2 %copy-start.3 = (f32[8,2,1024]{2,1,0:T(2,128)S(1)}, f32[8,2,1024]{2,1,0:T(2,128)}, u32[]{:S(2)}) copy-start(f32[8,2,1024]{2,1,0:T(2,128)} %param.15) | copy-start | bytes 196612
  0.0 17.0 %copy-start.1 = (s32[8,2,1024]{2,1,0:T(2,128)S(1)}, s32[8,2,1024]{2,1,0:T(2,128)}, u32[]{:S(2)}) copy-start(s32[8,2,1024]{2,1,0:T(2,128)} %param.17) | copy-start | bytes 196612
  0.0 17.2 %copy-start.2 = (f32[8,2,1024]{2,1,0:T(2,128)S(1)}, f32[8,2,1024]{2,1,0:T(2,128)}, u32[]{:S(2)}) copy-start(f32[8,2,1024]{2,1,0:T(2,128)} %param.14) | copy-start | bytes 196612
  0.0 17.3 %copy-start.4 = (f32[8,2,1024]{2,1,0:T(2,128)S(1)}, f32[8,2,1024]{2,1,0:T(2,128)}, u32[]{:S(2)}) copy-start(f32[8,2,1024]{2,1,0:T(2,128)} %param.16) | copy-start | bytes 196612
  1.1 16.5 %copy-start.5 = (f32[8,2,1024]{2,1,0:T(2,128)S(1)}, f32[8,2,1024]{2,1,0:T(2,128)}, u32[]{:S(2)}) copy-start(f32[8,2,1024]{2,1,0:T(2,128)} %param.18) | copy-start | bytes 196612
  3.8 18.3 %collective-permute-start = (f32[8,8,1,1024]{3,1,2,0:T(8,128)S(1)}, f32[8,8,1,1024]{3,1,2,0:T(8,128)S(1)}, u32[]{:S(2)}, u32[]{:S(2)}) collective-permute-start(f32[8,8,1,1024]{3,1,2,0:T(8,128)S(1)} %get-tuple-element.149), channel_id=1, source_target_pairs={{0,8},{8,16},{16,24},{24,32},{32,40},{40,48},{48,56},{56,64},{64,7... | collective-permute-start | bytes 786440 | tf_op jit(solution)/shard_map/ppermute | solution.py:15
  8.1 15.6 %copy-start = (f32[3,8,2,1024]{3,2,1,0:T(2,128)S(1)}, f32[3,8,2,1024]{3,2,1,0:T(2,128)}, u32[]{:S(2)}) copy-start(f32[3,8,2,1024]{3,2,1,0:T(2,128)} %param.13) | copy-start | bytes 589828
  8.1 15.5 %collective-permute-start.1 = (f32[8,8,1,1024]{3,1,2,0:T(8,128)S(1)}, f32[8,8,1,1024]{3,1,2,0:T(8,128)S(1)}, u32[]{:S(2)}, u32[]{:S(2)}) collective-permute-start(f32[8,8,1,1024]{3,1,2,0:T(8,128)S(1)} %get-tuple-element.150), channel_id=1, source_target_pairs={{8,0},{16,8},{24,16},{32,24},{40,32},{48,40},{56,48},{64,56},{72,6... | collective-permute-start | bytes 786440 | tf_op jit(solution)/shard_map/ppermute | solution.py:15
  28.7 26.2 %copy-start.7 = (s32[2,1]{0,1:T(1,128)S(1)}, s32[2,1]{0,1:T(1,128)}, u32[]{:S(2)}) copy-start(s32[2,1]{0,1:T(1,128)} %param.19) | copy-start | bytes 28
  37.6 38.7 %all-to-all-start = ((f32[8,1,8192]{2,1,0:T(1,128)}), f32[8,1,8192]{2,1,0:T(1,128)S(1)}, u32[]{:S(2)}, u32[]{:S(2)}) async-start(f32[8,1,8192]{2,1,0:T(1,128)} %reshape.151), calls=%async_computation | async-start | bytes 524288 | tf_op jit(solution)/shard_map/all_to_all | solution.py:162
  91.6 18.6 %copy-start.6 = (f32[2,64]{1,0:T(2,128)S(1)}, f32[2,64]{1,0:T(2,128)}, u32[]{:S(2)}) copy-start(f32[2,64]{1,0:T(2,128)} %param.20) | copy-start | bytes 1540
  91.6 18.6 %copy-start.8 = (f32[64]{0:T(128)S(1)}, f32[64]{0:T(128)}, u32[]{:S(2)}) copy-start(f32[64]{0:T(128)} %param.21) | copy-start | bytes 772
where the time goes:
time: 117 us; the launch traced here: 116 us
  local copies, waits for them, and re-layouts  32.6 us (28%)
  starting transfers between devices  30.4 us (26%)
  waiting for transfers between devices  27.3 us (23%)
  matrix products  21.7 us (19%)
  other arithmetic  3.61 us (3%)
    all_to_all x1, waiting for transfers between devices, local(): lax.all_to_all(packed, 'lev', split_axis=3, concat_axis=1, tiled=True)  21.3 us
    unnamed x25, local copies, waits for them, and re-layouts  20.1 us
    all_to_all x1, starting transfers between devices, local(): lax.all_to_all(packed, 'lev', split_axis=3, concat_axis=1, tiled=True)  17.3 us
    dot_general x2, matrix products, regrid_column(): jnp.einsum('kjc,fjc->fkc', intersection, layer_fields, precision=lax.Prec...  16.7 us
    ppermute x2, starting transfers between devices, passed_along(): return lax.ppermute(x, axis, pairs)  13.1 us
    ppermute x2, waiting for transfers between devices, passed_along(): return lax.ppermute(x, axis, pairs)  5.94 us
    all_to_all x2, local copies, waits for them, and re-layouts, local(): lax.all_to_all(packed, 'lev', split_axis=3, concat_axis=1, tiled=True)  5.69 us
    dot_general x2, matrix products, shortwave(): jnp.einsum('km,bmc->bkc', triangle, optical, precision=lax.Precision.HIGH...  5.09 us
  transfers between devices with their start and end apart: 3, of which 3 were waited for; matrix products, arithmetic and copies ran while one was open for 1% of the time, Pallas kernels for 0%

commit v1 on v0

v1 whole, which is shorter than its diff:
```python
import math

import jax
import jax.numpy as jnp
from jax import lax
from jax.experimental import pallas as pl
from jax.experimental.pallas import tpu as pltpu
from jax.sharding import PartitionSpec as P

lw_rate = 0.2
lw_damp = 0.1
LANES = 128
least_thick = 0.5
most_thick = 2.0
kernel_vmem = 8 * 1024 * 1024


def passed_along(x, axis, by):
    size = lax.axis_size(axis)
    pairs = [(i, i + by) for i in range(size) if 0 <= i + by < size]
    return lax.ppermute(x, axis, pairs)


def block_rows(x):
    lead, (levels, rows, cols) = x.shape[:-3], x.shape[-3:]
    x = x.reshape(*lead, levels, rows, cols // LANES, LANES)
    return jnp.swapaxes(x, -3, -2).reshape(*lead, levels * rows * cols // LANES, LANES)


def row_of(ref, row, levels, blocks, lead=()):
    return jnp.concatenate(
        [ref[(*lead, pl.ds(2 * b + row, levels, stride=2 * blocks), slice(None))] for b in range(blocks)],
        axis=1,
    )


def slope_weights(code):
    wb = jnp.where(code == 1, 1.0, jnp.where(code == 3, 0.5, 0.0))
    wf = jnp.where(code == 2, 1.0, jnp.where(code == 3, 0.5, 0.0))
    return wb, wf


def pack_body(levels, blocks, fields, north, south, limiter, up, down):
    nc = row_of(north, 1, levels, blocks)
    wb, wf = slope_weights(row_of(limiter, 1, levels, blocks))
    gain = nc * (0.5 * (1.0 - nc))
    up[6] = gain * wf
    sc = row_of(south, 0, levels, blocks)
    vb, vf = slope_weights(row_of(limiter, 0, levels, blocks))
    loss = sc * (0.5 * (1.0 - sc))
    down[6] = loss * vb
    for f in range(3):
        low = row_of(fields, 0, levels, blocks, (f,))
        top = row_of(fields, 1, levels, blocks, (f,))
        step = top - low
        up[f] = top
        up[3 + f] = nc * top + gain * (wb * step - wf * top)
        down[f] = low
        down[3 + f] = sc * low - loss * (vb * low + vf * step)


def advect_body(levels, blocks, fields, north, south, east, limiter, thick, below, above, out):
    lane = lax.broadcasted_iota(jnp.int32, (levels, blocks * LANES), 1)
    cols = blocks * LANES
    weights, rise_gain, sink_gain, ncs, scs = [], [], [], [], []
    for r in range(2):
        weights.append(slope_weights(row_of(limiter, r, levels, blocks)))
        nc = row_of(north, r, levels, blocks)
        sc = row_of(south, r, levels, blocks)
        ncs.append(nc)
        scs.append(sc)
        rise_gain.append(nc * (0.5 * (1.0 - nc)))
        sink_gain.append(sc * (0.5 * (1.0 - sc)))
    ecs = [row_of(east, r, levels, blocks) for r in range(2)]
    east_gain = [ec * (0.5 * (1.0 - ec)) for ec in ecs]
    for f in range(3):
        rows = [row_of(fields, r, levels, blocks, (f,)) for r in range(2)]
        before = below[f]
        after = above[f]
        diffs = [rows[0] - before, rows[1] - rows[0], after - rows[1]]
        rise, sink, kept = [], [], []
        for r in range(2):
            wb, wf = weights[r]
            slope = wb * diffs[r] + wf * diffs[r + 1]
            rise.append(ncs[r] * rows[r] + rise_gain[r] * slope)
            sink.append(scs[r] * rows[r] - sink_gain[r] * slope)
            step = rows[r] - pltpu.roll(rows[r], 1, 1)
            zonal = wb * step + wf * pltpu.roll(step, cols - 1, 1)
            going = ecs[r] * rows[r] + east_gain[r] * zonal
            kept.append(rows[r] - (going - pltpu.roll(going, 1, 1)))
        from_below = below[3 + f] + below[6] * rows[0]
        from_above = above[3 + f] + above[6] * rows[1]
        first = kept[0] - (rise[0] + sink[0]) + (from_below + sink[1])
        second = kept[1] - (rise[1] + sink[1]) + (rise[0] + from_above)
        for r, value in enumerate((first, second)):
            for b in range(blocks):
                out[b, pl.ds((r * 4 + f) * levels, levels), :] = value[:, b * LANES : (b + 1) * LANES]
    for r in range(2):
        for b in range(blocks):
            out[b, pl.ds((r * 4 + 3) * levels, levels), :] = thick[pl.ds(2 * b + r, levels, stride=2 * blocks), :]


def reach(first, last, levels):
    ratio = most_thick / least_thick
    lo, hi = first / levels, last / levels
    low = levels * lo / (ratio - (ratio - 1.0) * lo)
    high = levels * ratio * hi / (1.0 + (ratio - 1.0) * hi)
    return max(0, math.floor(low) - 1), min(levels, math.ceil(high) + 1)


def column_body(sources, per, bands, got, lit, absorb, flux, out, thick_s, low_s, top_s, adv_s, pad_s):
    levels = sources * per
    cols = LANES
    for r in range(2):
        for s in range(sources):
            for f in range(3):
                adv_s[r, f, pl.ds(s * per, per), :] = got[s, pl.ds((r * 4 + f) * per, per), :]
            thick_s[r, pl.ds(s * per, per), :] = got[s, pl.ds((r * 4 + 3) * per, per), :]
    at_row = lax.broadcasted_iota(jnp.int32, (levels, levels), 0)
    at_col = lax.broadcasted_iota(jnp.int32, (levels, levels), 1)
    triangle = jnp.where(at_row >= at_col, 1.0, 0.0).astype(jnp.float32)

    def running(x):
        return jnp.dot(triangle, x, precision=lax.Precision.HIGHEST, preferred_element_type=jnp.float32)

    thick = jnp.concatenate([thick_s[0], thick_s[1]], axis=1)
    top = running(thick)
    low = top - thick
    step = 8
    depths, inverse = [], []
    for r in range(2):
        top_s[r] = top[:, r * cols : (r + 1) * cols]
        low_s[r] = low[:, r * cols : (r + 1) * cols]
        depth = top_s[r, pl.ds(levels - 1, 1), :] * (1.0 / levels)
        depths.append(depth)
        inverse.append(1.0 / depth)
    sub = lax.broadcasted_iota(jnp.int32, (step, cols), 0).astype(jnp.float32)
    squares = [[], []]
    for r in range(2):
        depth8 = jnp.broadcast_to(depths[r], (step, cols))
        inv8 = jnp.broadcast_to(inverse[r], (step, cols))
        for k in range(0, levels, step):
            start, stop = reach(k, k + step, levels)
            bottom = (sub + float(k)) * depth8
            ceiling = (sub + float(k + 1)) * depth8
            sums = [jnp.zeros((step, cols), jnp.float32)] * 3
            for j in range(start, stop):
                edge_top = jnp.broadcast_to(top_s[r, pl.ds(j, 1), :], (step, cols))
                edge_low = jnp.broadcast_to(low_s[r, pl.ds(j, 1), :], (step, cols))
                shared = jnp.maximum(jnp.minimum(edge_top, ceiling) - jnp.maximum(edge_low, bottom), 0.0)
                for f in range(3):
                    sums[f] = sums[f] + shared * jnp.broadcast_to(adv_s[r, f, pl.ds(j, 1), :], (step, cols))
            values = [total * inv8 for total in sums]
            pad_s[r, pl.ds(step + k, step), :] = values[0]
            out[1, pl.ds(2 * k + r, step, stride=2), :] = values[1]
            out[2, pl.ds(2 * k + r, step, stride=2), :] = values[2]
            squares[r].append((values[1] * values[1] * depth8, values[2] * values[2] * depth8))
    stacked = jnp.concatenate(
        [jnp.concatenate([s[i] for s in squares[r]], axis=0) for r in range(2) for i in range(2)], axis=1
    )
    path = running(stacked)
    log2e = 1.4426950408889634
    paths = [path[:, i * cols : (i + 1) * cols] for i in range(4)]

    def one_band(b, sums):
        a0 = absorb[0, b] * (-log2e)
        a1 = absorb[1, b] * (-log2e)
        power = flux[b]
        return tuple(
            sums[r] + power * jnp.exp2(a0 * paths[2 * r] + a1 * paths[2 * r + 1]) for r in range(2)
        )

    zero = jnp.zeros((levels, cols), jnp.float32)
    light = (zero, zero)
    for b in range(bands):
        light = one_band(b, light)
    full = flux[0]
    for b in range(1, bands):
        full = full + flux[b]
    for r in range(2):
        top_s[r] = light[r]
        for s in range(0, levels, step):
            if s == 0:
                upper = jnp.concatenate([jnp.full((1, cols), full, jnp.float32), light[r][: step - 1]], axis=0)
            else:
                upper = top_s[r, pl.ds(s - 1, step), :]
            pad_s[2 + r, pl.ds(s, step), :] = upper
        pad_s[r, pl.ds(0, step), :] = jnp.zeros((step, cols), jnp.float32)
        pad_s[r, pl.ds(step + levels, step), :] = jnp.zeros((step, cols), jnp.float32)
        absorbed = (pad_s[2 + r, pl.ds(0, levels), :] - light[r]) * inverse[r]
        heat = absorbed * lit[r].astype(jnp.float32)
        here = pad_s[r, pl.ds(step, levels), :]
        beneath = pad_s[r, pl.ds(step - 1, levels), :]
        overlying = pad_s[r, pl.ds(step + 1, levels), :]
        cooling = lw_rate * (beneath + overlying - 2.0 * here) - lw_damp * here
        out[0, pl.ds(r, levels, stride=2), :] = here + (heat + cooling)


def local(fields, north, south, east, limiter, thickness, sunlit, absorb, solar_flux):
    _, levels, _, cols = fields.shape
    blocks = cols // LANES
    sources = lax.axis_size("lev")
    vmem = pl.BlockSpec(memory_space=pltpu.VMEM)
    smem = pl.BlockSpec(memory_space=pltpu.SMEM)
    fields_v, north_v, south_v, east_v, limiter_v, thick_v = (
        block_rows(x) for x in (fields, north, south, east, limiter, thickness)
    )
    halo = jax.ShapeDtypeStruct((7, levels, cols), jnp.float32)
    up, down = pl.pallas_call(
        lambda *refs: pack_body(levels, blocks, *refs),
        out_shape=(halo, halo),
        in_specs=[vmem] * 4,
        out_specs=(vmem, vmem),
        compiler_params=pltpu.CompilerParams(vmem_limit_bytes=kernel_vmem),
        name="pack",
    )(fields_v, north_v, south_v, limiter_v)
    below = passed_along(up, "lat", 1)
    above = passed_along(down, "lat", -1)
    pieces = pl.pallas_call(
        lambda *refs: advect_body(levels, blocks, *refs),
        out_shape=jax.ShapeDtypeStruct((blocks, 8 * levels, LANES), jnp.float32),
        in_specs=[vmem] * 8,
        out_specs=vmem,
        compiler_params=pltpu.CompilerParams(vmem_limit_bytes=kernel_vmem),
        name="advect",
    )(fields_v, north_v, south_v, east_v, limiter_v, thick_v, below, above)
    got = lax.all_to_all(pieces, "lev", 0, 0)
    whole = sources * levels
    result = pl.pallas_call(
        lambda *refs: column_body(sources, levels, absorb.shape[1], *refs),
        out_shape=jax.ShapeDtypeStruct((3, whole * 2, LANES), jnp.float32),
        in_specs=[vmem, smem, smem, smem],
        out_specs=vmem,
        scratch_shapes=[
            pltpu.VMEM((2, whole, LANES), jnp.float32),
            pltpu.VMEM((2, whole, LANES), jnp.float32),
            pltpu.VMEM((2, whole, LANES), jnp.float32),
            pltpu.VMEM((2, 3, whole, LANES), jnp.float32),
            pltpu.VMEM((4, whole + 16, LANES), jnp.float32),
        ],
        compiler_params=pltpu.CompilerParams(vmem_limit_bytes=kernel_vmem),
        name="column",
    )(got, sunlit.reshape(-1), absorb, solar_flux)
    return result.reshape(3, whole, 2, LANES)


def solution(mesh):
    in_specs = (
        P(None, "lev", "lat", None),
        P("lev", "lat", None),
        P("lev", "lat", None),
        P("lev", "lat", None),
        P("lev", "lat", None),
        P("lev", "lat", None),
        P("lat", "lev"),
        P(),
        P(),
    )
    out_specs = P(None, None, "lat", "lev")
    return jax.shard_map(local, mesh=mesh, in_specs=in_specs, out_specs=out_specs, check_vma=False)
```

time: 117 us -> 66.5 us (0.57)
  the two profiles are of different devices: /device:TPU:6 before, /device:TPU:26 now
where the time goes in v1:
time: 66.5 us; the launch traced here: 66.1 us
  blocking collectives  39.6 us (60%)
  starting transfers between devices  9.7 us (15%)
  waiting for transfers between devices  8.69 us (13%)
  local copies, waits for them, and re-layouts  4.13 us (6%)
  Pallas kernels  3.92 us (6%)
    all_to_all x1, blocking collectives, local(): got = lax.all_to_all(pieces, 'lev', 0, 0)  39.6 us
    ppermute x2, starting transfers between devices, passed_along(): return lax.ppermute(x, axis, pairs)  9.7 us
    ppermute x2, waiting for transfers between devices, passed_along(): return lax.ppermute(x, axis, pairs)  8.69 us
    unnamed x18, local copies, waits for them, and re-layouts  4.13 us
    pallas_call x1, Pallas kernels, local(): pl.pallas_call(lambda *refs: column_body(sources, levels, absorb.shape[1]...  3.4 us
  transfers between devices with their start and end apart: 2, of which 2 were waited for; matrix products, arithmetic and copies ran while one was open for 0% of the time, Pallas kernels for 0%

profile of v1, /device:TPU:26, one launch (start us, length us, event | category | flops | bytes accessed | tf_op | source)
XLA Modules:
  0.0 66.1 jit_solution(2487755263959401570)
XLA Ops:
  0.0 0.0 copy-start
  0.0 0.9 %copy-done = f32[3,8,2,1024]{3,2,1,0:T(2,128)S(1)} copy-done((f32[3,8,2,1024]{3,2,1,0:T(2,128)S(1)}, f32[3,8,2,1024]{3,2,1,0:T(2,128)}, u32[]{:S(2)}) %copy-start) | copy-done | bytes 196632
  0.9 0.0 copy-start.1
  0.9 0.8 %copy-done.1 = f32[8,2,1024]{2,1,0:T(2,128)S(1)} copy-done((f32[8,2,1024]{2,1,0:T(2,128)S(1)}, f32[8,2,1024]{2,1,0:T(2,128)}, u32[]{:S(2)}) %copy-start.1) | copy-done | bytes 65560
  1.8 0.0 copy-start.2
  1.8 0.8 %copy-done.2 = f32[8,2,1024]{2,1,0:T(2,128)S(1)} copy-done((f32[8,2,1024]{2,1,0:T(2,128)S(1)}, f32[8,2,1024]{2,1,0:T(2,128)}, u32[]{:S(2)}) %copy-start.2) | copy-done | bytes 65560
  2.6 0.0 copy-start.3
  2.6 0.8 %copy-done.3 = s32[8,2,1024]{2,1,0:T(2,128)S(1)} copy-done((s32[8,2,1024]{2,1,0:T(2,128)S(1)}, s32[8,2,1024]{2,1,0:T(2,128)}, u32[]{:S(2)}) %copy-start.3) | copy-done | bytes 65560
  3.4 0.0 copy-start.4
  3.5 0.0 copy-start.5
  3.5 0.1 pack.1
  3.6 4.3 %collective-permute-start = (f32[7,8,1024]{2,1,0:T(8,128)S(1)}, f32[7,8,1024]{2,1,0:T(8,128)S(1)}, u32[]{:S(2)}, u32[]{:S(2)}) collective-permute-start(f32[7,8,1024]{2,1,0:T(8,128)S(1)} %get-tuple-element.7), channel_id=1, source_target_pairs={{0,8},{8,16},{16,24},{24,32},{32,40},{40,48},{48,56},{56,64},{64,7... | collective-permute-start | bytes 688136 | tf_op jit(solution)/shard_map/ppermute | solution.py:21
  7.9 5.4 %collective-permute-start.1 = (f32[7,8,1024]{2,1,0:T(8,128)S(1)}, f32[7,8,1024]{2,1,0:T(8,128)S(1)}, u32[]{:S(2)}, u32[]{:S(2)}) collective-permute-start(f32[7,8,1024]{2,1,0:T(8,128)S(1)} %get-tuple-element.8), channel_id=1, source_target_pairs={{8,0},{16,8},{24,16},{32,24},{40,32},{48,40},{56,48},{64,56},{72,6... | collective-permute-start | bytes 688136 | tf_op jit(solution)/shard_map/ppermute | solution.py:21
  13.3 4.6 %collective-permute-done.refs_6_ = f32[7,8,1024]{2,1,0:T(8,128)S(1)} collective-permute-done((f32[7,8,1024]{2,1,0:T(8,128)S(1)}, f32[7,8,1024]{2,1,0:T(8,128)S(1)}, u32[]{:S(2)}, u32[]{:S(2)}) %collective-permute-start) | collective-permute-done | bytes 229408 | tf_op jit(solution)/shard_map/ppermute | solution.py:21
  17.9 4.1 %collective-permute-done.1.refs_7_ = f32[7,8,1024]{2,1,0:T(8,128)S(1)} collective-permute-done((f32[7,8,1024]{2,1,0:T(8,128)S(1)}, f32[7,8,1024]{2,1,0:T(8,128)S(1)}, u32[]{:S(2)}, u32[]{:S(2)}) %collective-permute-start.1) | collective-permute-done | bytes 229408 | tf_op jit(solution)/shard_map/ppermute | solution.py:21
  22.0 0.0 copy-done.4
  22.0 0.0 copy-done.5
  22.0 0.4 advect.1
  22.4 0.0 copy-start.8
  22.4 39.6 %all_to_all.5.refs_0_ = f32[8,64,128]{2,1,0:T(8,128)S(1)} all-to-all(f32[8,64,128]{2,1,0:T(8,128)S(1)} %advect.1), channel_id=1, replica_groups=mesh['lat'=128,'lev'=8] {'lev'}, dimensions={0} | all-to-all | bytes 524288 | tf_op jit(solution)/shard_map/all_to_all | solution.py:227
  62.0 0.0 copy-start.6
  62.0 0.0 copy-start.7
  62.0 0.0 copy-done.8
  62.1 0.7 %copy-done.6 = f32[2,64]{1,0:T(2,128)S(1)} copy-done((f32[2,64]{1,0:T(2,128)S(1)}, f32[2,64]{1,0:T(2,128)}, u32[]{:S(2)}) %copy-start.6) | copy-done | bytes 536
  62.7 0.0 copy-done.7
  62.7 3.4 %column.1 = f32[3,128,128]{2,1,0:T(8,128)} custom-call(f32[8,64,128]{2,1,0:T(8,128)S(1)} %all_to_all.5.refs_0_, s32[2]{0:T(128)S(1)} %bitcast.42, f32[2,64]{1,0:T(2,128)S(1)} %copy-done.6, f32[64]{0:T(128)S(1)} %copy-done.8), custom_call_target="tpu_custom_call" | custom-call | tf_op jit(solution)/shard_map/column/pallas_call | solution.py:229
Async XLA Ops:
  0.0 0.9 %copy-start = (f32[3,8,2,1024]{3,2,1,0:T(2,128)S(1)}, f32[3,8,2,1024]{3,2,1,0:T(2,128)}, u32[]{:S(2)}) copy-start(f32[3,8,2,1024]{3,2,1,0:T(2,128)} %param.9) | copy-start | bytes 589828
  0.9 0.8 %copy-start.1 = (f32[8,2,1024]{2,1,0:T(2,128)S(1)}, f32[8,2,1024]{2,1,0:T(2,128)}, u32[]{:S(2)}) copy-start(f32[8,2,1024]{2,1,0:T(2,128)} %param.10) | copy-start | bytes 196612
  1.8 0.8 %copy-start.2 = (f32[8,2,1024]{2,1,0:T(2,128)S(1)}, f32[8,2,1024]{2,1,0:T(2,128)}, u32[]{:S(2)}) copy-start(f32[8,2,1024]{2,1,0:T(2,128)} %param.11) | copy-start | bytes 196612
  2.6 0.8 %copy-start.3 = (s32[8,2,1024]{2,1,0:T(2,128)S(1)}, s32[8,2,1024]{2,1,0:T(2,128)}, u32[]{:S(2)}) copy-start(s32[8,2,1024]{2,1,0:T(2,128)} %param.13) | copy-start | bytes 196612
  3.4 18.6 %copy-start.4 = (f32[8,2,1024]{2,1,0:T(2,128)S(1)}, f32[8,2,1024]{2,1,0:T(2,128)}, u32[]{:S(2)}) copy-start(f32[8,2,1024]{2,1,0:T(2,128)} %param.12) | copy-start | bytes 196612
  3.5 18.6 %copy-start.5 = (f32[8,2,1024]{2,1,0:T(2,128)S(1)}, f32[8,2,1024]{2,1,0:T(2,128)}, u32[]{:S(2)}) copy-start(f32[8,2,1024]{2,1,0:T(2,128)} %param.14) | copy-start | bytes 196612
  3.6 14.3 %collective-permute-start = (f32[7,8,1024]{2,1,0:T(8,128)S(1)}, f32[7,8,1024]{2,1,0:T(8,128)S(1)}, u32[]{:S(2)}, u32[]{:S(2)}) collective-permute-start(f32[7,8,1024]{2,1,0:T(8,128)S(1)} %get-tuple-element.7), channel_id=1, source_target_pairs={{0,8},{8,16},{16,24},{24,32},{32,40},{40,48},{48,56},{56,64},{64,7... | collective-permute-start | bytes 688136 | tf_op jit(solution)/shard_map/ppermute | solution.py:21
  7.9 14.1 %collective-permute-start.1 = (f32[7,8,1024]{2,1,0:T(8,128)S(1)}, f32[7,8,1024]{2,1,0:T(8,128)S(1)}, u32[]{:S(2)}, u32[]{:S(2)}) collective-permute-start(f32[7,8,1024]{2,1,0:T(8,128)S(1)} %get-tuple-element.8), channel_id=1, source_target_pairs={{8,0},{16,8},{24,16},{32,24},{40,32},{48,40},{56,48},{64,56},{72,6... | collective-permute-start | bytes 688136 | tf_op jit(solution)/shard_map/ppermute | solution.py:21
  22.4 39.7 %copy-start.8 = (f32[64]{0:T(128)S(1)}, f32[64]{0:T(128)}, u32[]{:S(2)}) copy-start(f32[64]{0:T(128)} %refs_3_.1) | copy-start | bytes 772
  62.0 0.7 %copy-start.6 = (f32[2,64]{1,0:T(2,128)S(1)}, f32[2,64]{1,0:T(2,128)}, u32[]{:S(2)}) copy-start(f32[2,64]{1,0:T(2,128)} %refs_2_.1) | copy-start | bytes 1540
  62.0 0.7 %copy-start.7 = (s32[2,1]{0,1:T(1,128)S(1)}, s32[2,1]{0,1:T(1,128)}, u32[]{:S(2)}) copy-start(s32[2,1]{0,1:T(1,128)} %param.15) | copy-start | bytes 28

commit v2 on v1

--- a/solution.py
+++ b/solution.py
@@ -13,12 +13,7 @@
 least_thick = 0.5
 most_thick = 2.0
 kernel_vmem = 8 * 1024 * 1024
-
-
-def passed_along(x, axis, by):
-    size = lax.axis_size(axis)
-    pairs = [(i, i + by) for i in range(size) if 0 <= i + by < size]
-    return lax.ppermute(x, axis, pairs)
+log2e = 1.4426950408889634
 
 
 def block_rows(x):
@@ -40,27 +35,57 @@
     return wb, wf
 
 
-def pack_body(levels, blocks, fields, north, south, limiter, up, down):
-    nc = row_of(north, 1, levels, blocks)
-    wb, wf = slope_weights(row_of(limiter, 1, levels, blocks))
-    gain = nc * (0.5 * (1.0 - nc))
-    up[6] = gain * wf
-    sc = row_of(south, 0, levels, blocks)
-    vb, vf = slope_weights(row_of(limiter, 0, levels, blocks))
-    loss = sc * (0.5 * (1.0 - sc))
-    down[6] = loss * vb
-    for f in range(3):
-        low = row_of(fields, 0, levels, blocks, (f,))
-        top = row_of(fields, 1, levels, blocks, (f,))
-        step = top - low
-        up[f] = top
-        up[3 + f] = nc * top + gain * (wb * step - wf * top)
-        down[f] = low
-        down[3 + f] = sc * low - loss * (vb * low + vf * step)
-
-
-def advect_body(levels, blocks, fields, north, south, east, limiter, thick, below, above, out):
-    lane = lax.broadcasted_iota(jnp.int32, (levels, blocks * LANES), 1)
+def pack_body(levels, blocks, *refs):
+    sources, near, far, held, sems = refs[:6], refs[6], refs[7], refs[8:14], refs[14]
+    copies = [pltpu.make_async_copy(src, dst, sems.at[i]) for i, (src, dst) in enumerate(zip(sources, held))]
+    for copy in copies:
+        copy.start()
+    for copy in copies[:4]:
+        copy.wait()
+    fields, north, south, limiter = held[:4]
+
+    def pack(up, down):
+        nc = row_of(north, 1, levels, blocks)
+        wb, wf = slope_weights(row_of(limiter, 1, levels, blocks))
+        gain = nc * (0.5 * (1.0 - nc))
+        up[6] = gain * wf
+        sc = row_of(south, 0, levels, blocks)
+        vb, vf = slope_weights(row_of(limiter, 0, levels, blocks))
+        loss = sc * (0.5 * (1.0 - sc))
+        down[6] = loss * vb
+        for f in range(3):
+            low = row_of(fields, 0, levels, blocks, (f,))
+            top = row_of(fields, 1, levels, blocks, (f,))
+            step = top - low
+            up[f] = top
+            up[3 + f] = nc * top + gain * (wb * step - wf * top)
+            down[f] = low
+            down[3 + f] = sc * low - loss * (vb * low + vf * step)
+
+    odd = lax.rem(lax.axis_index("lat"), 2) == 1
+    pl.when(jnp.logical_not(odd))(lambda: pack(near, far))
+    pl.when(odd)(lambda: pack(far, near))
+    for copy in copies[4:]:
+        copy.wait()
+
+
+def prepare_body(bands, lit, absorb, flux, powers, daylight):
+    for b in range(bands):
+        powers[pl.ds(b, 1), :] = jnp.full((1, LANES), absorb[0, b] * (-log2e), jnp.float32)
+        powers[pl.ds(bands + b, 1), :] = jnp.full((1, LANES), absorb[1, b] * (-log2e), jnp.float32)
+        powers[pl.ds(2 * bands + b, 1), :] = jnp.full((1, LANES), flux[b], jnp.float32)
+    for r in range(2):
+        daylight[r] = jnp.full((8, LANES), lit[r].astype(jnp.float32), jnp.float32)
+
+
+def advect_body(levels, blocks, *refs):
+    near, far = refs[6:8]
+    odd = lax.rem(lax.axis_index("lat"), 2) == 1
+    pl.when(jnp.logical_not(odd))(lambda: advect(levels, blocks, *refs[:6], far, near, refs[10]))
+    pl.when(odd)(lambda: advect(levels, blocks, *refs[:6], near, far, refs[10]))
+
+
+def advect(levels, blocks, fields, north, south, limiter, east, thick, below, above, out):
     cols = blocks * LANES
     weights, rise_gain, sink_gain, ncs, scs = [], [], [], [], []
     for r in range(2):
@@ -108,7 +133,7 @@
     return max(0, math.floor(low) - 1), min(levels, math.ceil(high) + 1)
 
 
-def column_body(sources, per, bands, got, lit, absorb, flux, out, thick_s, low_s, top_s, adv_s, pad_s):
+def column_body(sources, per, bands, got, powers, daylight, out_h, thick_s, low_s, top_s, adv_s, pad_s, out, sems):
     levels = sources * per
     cols = LANES
     for r in range(2):
@@ -155,92 +180,105 @@
             out[1, pl.ds(2 * k + r, step, stride=2), :] = values[1]
             out[2, pl.ds(2 * k + r, step, stride=2), :] = values[2]
             squares[r].append((values[1] * values[1] * depth8, values[2] * values[2] * depth8))
+    copies = [pltpu.make_async_copy(out.at[f], out_h.at[f], sems.at[f]) for f in range(3)]
+    copies[1].start()
+    copies[2].start()
     stacked = jnp.concatenate(
         [jnp.concatenate([s[i] for s in squares[r]], axis=0) for r in range(2) for i in range(2)], axis=1
     )
     path = running(stacked)
-    log2e = 1.4426950408889634
     paths = [path[:, i * cols : (i + 1) * cols] for i in range(4)]
-
-    def one_band(b, sums):
-        a0 = absorb[0, b] * (-log2e)
-        a1 = absorb[1, b] * (-log2e)
-        power = flux[b]
-        return tuple(
-            sums[r] + power * jnp.exp2(a0 * paths[2 * r] + a1 * paths[2 * r + 1]) for r in range(2)
-        )
-
-    zero = jnp.zeros((levels, cols), jnp.float32)
-    light = (zero, zero)
+    light = [jnp.zeros((levels, cols), jnp.float32)] * 2
+    full = jnp.zeros((1, cols), jnp.float32)
     for b in range(bands):
-        light = one_band(b, light)
-    full = flux[0]
-    for b in range(1, bands):
-        full = full + flux[b]
+        a0 = jnp.broadcast_to(powers[pl.ds(b, 1), :], (levels, cols))
+        a1 = jnp.broadcast_to(powers[pl.ds(bands + b, 1), :], (levels, cols))
+        power = jnp.broadcast_to(powers[pl.ds(2 * bands + b, 1), :], (levels, cols))
+        full = full + powers[pl.ds(2 * bands + b, 1), :]
+        for r in range(2):
+            light[r] = light[r] + power * jnp.exp2(a0 * paths[2 * r] + a1 * paths[2 * r + 1])
     for r in range(2):
         top_s[r] = light[r]
-        for s in range(0, levels, step):
-            if s == 0:
-                upper = jnp.concatenate([jnp.full((1, cols), full, jnp.float32), light[r][: step - 1]], axis=0)
-            else:
-                upper = top_s[r, pl.ds(s - 1, step), :]
-            pad_s[2 + r, pl.ds(s, step), :] = upper
+        upper = [jnp.concatenate([full, light[r][: step - 1]], axis=0)]
+        upper += [top_s[r, pl.ds(s - 1, step), :] for s in range(step, levels, step)]
+        absorbed = (jnp.concatenate(upper, axis=0) - light[r]) * inverse[r]
+        heat = absorbed * daylight[r, pl.ds(0, 1), :]
         pad_s[r, pl.ds(0, step), :] = jnp.zeros((step, cols), jnp.float32)
         pad_s[r, pl.ds(step + levels, step), :] = jnp.zeros((step, cols), jnp.float32)
-        absorbed = (pad_s[2 + r, pl.ds(0, levels), :] - light[r]) * inverse[r]
-        heat = absorbed * lit[r].astype(jnp.float32)
         here = pad_s[r, pl.ds(step, levels), :]
         beneath = pad_s[r, pl.ds(step - 1, levels), :]
         overlying = pad_s[r, pl.ds(step + 1, levels), :]
         cooling = lw_rate * (beneath + overlying - 2.0 * here) - lw_damp * here
         out[0, pl.ds(r, levels, stride=2), :] = here + (heat + cooling)
+    copies[0].start()
+    for copy in copies:
+        copy.wait()
+
+
+def swapped(x, axis, first):
+    size = lax.axis_size(axis)
+    pairs = [(i, i + 1) for i in range(first, size - 1, 2)]
+    return lax.ppermute(x, axis, [way for i, j in pairs for way in ((i, j), (j, i))])
 
 
 def local(fields, north, south, east, limiter, thickness, sunlit, absorb, solar_flux):
     _, levels, _, cols = fields.shape
     blocks = cols // LANES
+    bands = absorb.shape[1]
     sources = lax.axis_size("lev")
     vmem = pl.BlockSpec(memory_space=pltpu.VMEM)
     smem = pl.BlockSpec(memory_space=pltpu.SMEM)
-    fields_v, north_v, south_v, east_v, limiter_v, thick_v = (
-        block_rows(x) for x in (fields, north, south, east, limiter, thickness)
-    )
+    hbm = pl.BlockSpec(memory_space=pltpu.HBM)
+    params = pltpu.CompilerParams(vmem_limit_bytes=kernel_vmem)
+    given = [pltpu.with_memory_space_constraint(block_rows(x), pltpu.HBM) for x in (fields, north, south, limiter, east, thickness)]
     halo = jax.ShapeDtypeStruct((7, levels, cols), jnp.float32)
-    up, down = pl.pallas_call(
+    near, far, *held = pl.pallas_call(
         lambda *refs: pack_body(levels, blocks, *refs),
-        out_shape=(halo, halo),
-        in_specs=[vmem] * 4,
+        out_shape=[halo, halo] + [jax.ShapeDtypeStruct(x.shape, x.dtype) for x in given],
+        in_specs=[hbm] * 6,
+        out_specs=[vmem] * 8,
+        scratch_shapes=[pltpu.SemaphoreType.DMA((6,))],
+        compiler_params=params,
+        name="pack",
+    )(*given)
+    far = swapped(far, "lat", 1)
+    near = swapped(near, "lat", 0)
+    powers, daylight = pl.pallas_call(
+        lambda *refs: prepare_body(bands, *refs),
+        out_shape=(jax.ShapeDtypeStruct((3 * bands, LANES), jnp.float32), jax.ShapeDtypeStruct((2, 8, LANES), jnp.float32)),
+        in_specs=[smem] * 3,
         out_specs=(vmem, vmem),
-        compiler_params=pltpu.CompilerParams(vmem_limit_bytes=kernel_vmem),
-        name="pack",
-    )(fields_v, north_v, south_v, limiter_v)
-    below = passed_along(up, "lat", 1)
-    above = passed_along(down, "lat", -1)
+        compiler_params=params,
+        cost_estimate=pl.CostEstimate(flops=100000, bytes_accessed=1000000, transcendentals=0),
+        name="prepare",
+    )(sunlit.reshape(-1), absorb, solar_flux)
     pieces = pl.pallas_call(
         lambda *refs: advect_body(levels, blocks, *refs),
         out_shape=jax.ShapeDtypeStruct((blocks, 8 * levels, LANES), jnp.float32),
-        in_specs=[vmem] * 8,
+        in_specs=[vmem] * 10,
         out_specs=vmem,
-        compiler_params=pltpu.CompilerParams(vmem_limit_bytes=kernel_vmem),
+        compiler_params=params,
         name="advect",
-    )(fields_v, north_v, south_v, east_v, limiter_v, thick_v, below, above)
+    )(*held, near, far, powers, daylight)
     got = lax.all_to_all(pieces, "lev", 0, 0)
     whole = sources * levels
     result = pl.pallas_call(
-        lambda *refs: column_body(sources, levels, absorb.shape[1], *refs),
+        lambda *refs: column_body(sources, levels, bands, *refs),
         out_shape=jax.ShapeDtypeStruct((3, whole * 2, LANES), jnp.float32),
-        in_specs=[vmem, smem, smem, smem],
-        out_specs=vmem,
+        in_specs=[vmem] * 3,
+        out_specs=hbm,
         scratch_shapes=[
             pltpu.VMEM((2, whole, LANES), jnp.float32),
             pltpu.VMEM((2, whole, LANES), jnp.float32),
             pltpu.VMEM((2, whole, LANES), jnp.float32),
             pltpu.VMEM((2, 3, whole, LANES), jnp.float32),
-            pltpu.VMEM((4, whole + 16, LANES), jnp.float32),
+            pltpu.VMEM((2, whole + 16, LANES), jnp.float32),
+            pltpu.VMEM((3, whole * 2, LANES), jnp.float32),
+            pltpu.SemaphoreType.DMA((3,)),
         ],
-        compiler_params=pltpu.CompilerParams(vmem_limit_bytes=kernel_vmem),
+        compiler_params=params,
         name="column",
-    )(got, sunlit.reshape(-1), absorb, solar_flux)
+    )(got, powers, daylight)
     return result.reshape(3, whole, 2, LANES)
 
 

time: 66.5 us -> 63 us (0.947)
  the two profiles are of different devices: /device:TPU:26 before, /device:TPU:56 now
where the time goes in v2:
time: 63 us; the launch traced here: 62.8 us
  blocking collectives  39 us (62%)
  starting transfers between devices  10.7 us (17%)
  waiting for transfers between devices  7.81 us (12%)
  Pallas kernels  5.14 us (8%)
    all_to_all x1, blocking collectives, local(): got = lax.all_to_all(pieces, 'lev', 0, 0)  39 us
    ppermute x2, starting transfers between devices, swapped(): lax.ppermute(x, axis, [way for i, j in pairs for way in ((i, j), (j, i))])  10.7 us
    ppermute x2, waiting for transfers between devices, swapped(): lax.ppermute(x, axis, [way for i, j in pairs for way in ((i, j), (j, i))])  7.81 us
    pallas_call x1, Pallas kernels, local(): pl.pallas_call(lambda *refs: column_body(sources, levels, bands, *refs),...  2.89 us
  transfers between devices with their start and end apart: 2, of which 1 were waited for; matrix products, arithmetic and copies ran while one was open for 0% of the time, Pallas kernels for 1%

profile of v2, /device:TPU:56, one launch (start us, length us, event | category | flops | bytes accessed | tf_op | source)
XLA Modules:
  0.0 62.8 jit_solution(60034246838288868)
XLA Ops:
  0.0 1.2 %pack.1 = (f32[7,8,1024]{2,1,0:T(8,128)S(1)}, f32[7,8,1024]{2,1,0:T(8,128)S(1)}, f32[3,128,128]{2,1,0:T(8,128)S(1)}, f32[128,128]{1,0:T(8,128)S(1)}, f32[128,128...) custom-call(f32[3,128,128]{2,1,0:T(8,128)} %bitcast.33, ...), custom_call_target="tpu_custom_call" | custom-call | tf_op jit(solution)/shard_map/pack/pallas_call | solution.py:235
  1.2 4.3 %collective-permute-start = (f32[7,8,1024]{2,1,0:T(8,128)S(1)}, f32[7,8,1024]{2,1,0:T(8,128)S(1)}, u32[]{:S(2)}, u32[]{:S(2)}) collective-permute-start(f32[7,8,1024]{2,1,0:T(8,128)S(1)} %get-tuple-element.21), channel_id=1, source_target_pairs={{0,8},{8,0},{16,24},{24,16},{32,40},{40,32},{48,56},{56,48},{64,72... | collective-permute-start | bytes 688136 | tf_op jit(solution)/shard_map/ppermute | solution.py:221
  5.5 0.0 copy-start.2
  5.5 0.0 copy-start
  5.5 0.0 copy-start.1
  5.5 6.5 %collective-permute-start.1 = (f32[7,8,1024]{2,1,0:T(8,128)S(1)}, f32[7,8,1024]{2,1,0:T(8,128)S(1)}, u32[]{:S(2)}, u32[]{:S(2)}) collective-permute-start(f32[7,8,1024]{2,1,0:T(8,128)S(1)} %get-tuple-element.22), channel_id=1, source_target_pairs={{8,16},{16,8},{24,32},{32,24},{40,48},{48,40},{56,64},{64,56},{72,... | collective-permute-start | bytes 688136 | tf_op jit(solution)/shard_map/ppermute | solution.py:221
  12.0 0.0 copy-done.2
  12.0 0.0 copy-done
  12.0 0.0 copy-done.1
  12.0 0.7 %prepare.1 = (f32[192,128]{1,0:T(8,128)S(1)}, f32[2,8,128]{2,1,0:T(8,128)S(1)}) custom-call(s32[2]{0:T(128)S(1)} %bitcast.32, f32[2,64]{1,0:T(2,128)S(1)} %copy-done, f32[64]{0:T(128)S(1)} %copy-done.2), custom_call_target="tpu_custom_call" | custom-call | flops 100000 | bytes 1000000 | tf_op jit(solution)/shard_map/prepare/pallas_call | solution.py:246
  12.7 0.0 collective-permute-done.refs_6_
  12.7 7.8 %collective-permute-done.1.refs_7_ = f32[7,8,1024]{2,1,0:T(8,128)S(1)} collective-permute-done((f32[7,8,1024]{2,1,0:T(8,128)S(1)}, f32[7,8,1024]{2,1,0:T(8,128)S(1)}, u32[]{:S(2)}, u32[]{:S(2)}) %collective-permute-start.1) | collective-permute-done | bytes 229408 | tf_op jit(solution)/shard_map/ppermute | solution.py:221
  20.5 0.4 advect.1
  20.9 39.0 %all_to_all.5.refs_0_ = f32[8,64,128]{2,1,0:T(8,128)S(1)} all-to-all(f32[8,64,128]{2,1,0:T(8,128)S(1)} %advect.1), channel_id=1, replica_groups=mesh['lat'=128,'lev'=8] {'lev'}, dimensions={0} | all-to-all | bytes 524288 | tf_op jit(solution)/shard_map/all_to_all | solution.py:263
  59.9 2.9 %column.1 = f32[3,128,128]{2,1,0:T(8,128)} custom-call(f32[8,64,128]{2,1,0:T(8,128)S(1)} %all_to_all.5.refs_0_, f32[192,128]{1,0:T(8,128)S(1)} %get-tuple-element.23.refs_8_.refs_1_, f32[2,8,128]{2,1,0:T(8,128)S(1)} %get-tuple-element.24.refs_9_.refs_2_), custom_call_target="tpu_custom_call" | custom-call | tf_op jit(solution)/shard_map/column/pallas_call | solution.py:265
Async XLA Ops:
  1.2 11.5 %collective-permute-start = (f32[7,8,1024]{2,1,0:T(8,128)S(1)}, f32[7,8,1024]{2,1,0:T(8,128)S(1)}, u32[]{:S(2)}, u32[]{:S(2)}) collective-permute-start(f32[7,8,1024]{2,1,0:T(8,128)S(1)} %get-tuple-element.21), channel_id=1, source_target_pairs={{0,8},{8,0},{16,24},{24,16},{32,40},{40,32},{48,56},{56,48},{64,72... | collective-permute-start | bytes 688136 | tf_op jit(solution)/shard_map/ppermute | solution.py:221
  5.5 6.5 %copy-start.2 = (f32[64]{0:T(128)S(1)}, f32[64]{0:T(128)}, u32[]{:S(2)}) copy-start(f32[64]{0:T(128)} %refs_2_.1) | copy-start | bytes 772
  5.5 6.5 %copy-start = (f32[2,64]{1,0:T(2,128)S(1)}, f32[2,64]{1,0:T(2,128)}, u32[]{:S(2)}) copy-start(f32[2,64]{1,0:T(2,128)} %refs_1_.1) | copy-start | bytes 1540
  5.5 6.5 %copy-start.1 = (s32[2,1]{0,1:T(1,128)S(1)}, s32[2,1]{0,1:T(1,128)}, u32[]{:S(2)}) copy-start(s32[2,1]{0,1:T(1,128)} %param.15) | copy-start | bytes 28
  5.5 15.0 %collective-permute-start.1 = (f32[7,8,1024]{2,1,0:T(8,128)S(1)}, f32[7,8,1024]{2,1,0:T(8,128)S(1)}, u32[]{:S(2)}, u32[]{:S(2)}) collective-permute-start(f32[7,8,1024]{2,1,0:T(8,128)S(1)} %get-tuple-element.22), channel_id=1, source_target_pairs={{8,16},{16,8},{24,32},{32,24},{40,48},{48,40},{56,64},{64,56},{72,... | collective-permute-start | bytes 688136 | tf_op jit(solution)/shard_map/ppermute | solution.py:221

commit v3 on v2

--- a/solution.py
+++ b/solution.py
@@ -6,6 +6,7 @@
 from jax.experimental import pallas as pl
 from jax.experimental.pallas import tpu as pltpu
 from jax.sharding import PartitionSpec as P
+
 
 lw_rate = 0.2
 lw_damp = 0.1
@@ -79,13 +80,20 @@
 
 
 def advect_body(levels, blocks, *refs):
-    near, far = refs[6:8]
-    odd = lax.rem(lax.axis_index("lat"), 2) == 1
-    pl.when(jnp.logical_not(odd))(lambda: advect(levels, blocks, *refs[:6], far, near, refs[10]))
-    pl.when(odd)(lambda: advect(levels, blocks, *refs[:6], near, far, refs[10]))
-
-
-def advect(levels, blocks, fields, north, south, limiter, east, thick, below, above, out):
+    core = lax.rem(lax.axis_index("lev"), 2)
+    pl.when(core == 0)(lambda: advect(levels, blocks, *refs[:8], refs[10], refs[11]))
+    pl.when(core == 1)(lambda: advect(levels, blocks, *refs[:8], refs[11], refs[10]))
+
+
+def advect(levels, blocks, fields, north, south, limiter, east, thick, near, far, even, odd):
+    above_far = lax.rem(lax.axis_index("lat"), 2) == 1
+
+    def below(i):
+        return jnp.where(above_far, near[i], far[i])
+
+    def above(i):
+        return jnp.where(above_far, far[i], near[i])
+
     cols = blocks * LANES
     weights, rise_gain, sink_gain, ncs, scs = [], [], [], [], []
     for r in range(2):
@@ -100,8 +108,8 @@
     east_gain = [ec * (0.5 * (1.0 - ec)) for ec in ecs]
     for f in range(3):
         rows = [row_of(fields, r, levels, blocks, (f,)) for r in range(2)]
-        before = below[f]
-        after = above[f]
+        before = below(f)
+        after = above(f)
         diffs = [rows[0] - before, rows[1] - rows[0], after - rows[1]]
         rise, sink, kept = [], [], []
         for r in range(2):
@@ -113,16 +121,27 @@
             zonal = wb * step + wf * pltpu.roll(step, cols - 1, 1)
             going = ecs[r] * rows[r] + east_gain[r] * zonal
             kept.append(rows[r] - (going - pltpu.roll(going, 1, 1)))
-        from_below = below[3 + f] + below[6] * rows[0]
-        from_above = above[3 + f] + above[6] * rows[1]
+        from_below = below(3 + f) + below(6) * rows[0]
+        from_above = above(3 + f) + above(6) * rows[1]
         first = kept[0] - (rise[0] + sink[0]) + (from_below + sink[1])
         second = kept[1] - (rise[1] + sink[1]) + (rise[0] + from_above)
         for r, value in enumerate((first, second)):
             for b in range(blocks):
-                out[b, pl.ds((r * 4 + f) * levels, levels), :] = value[:, b * LANES : (b + 1) * LANES]
+                out = (even, odd)[b % 2]
+                out[b // 2, pl.ds((r * 4 + f) * levels, levels), :] = value[:, b * LANES : (b + 1) * LANES]
     for r in range(2):
         for b in range(blocks):
-            out[b, pl.ds((r * 4 + 3) * levels, levels), :] = thick[pl.ds(2 * b + r, levels, stride=2 * blocks), :]
+            out = (even, odd)[b % 2]
+            out[b // 2, pl.ds((r * 4 + 3) * levels, levels), :] = thick[pl.ds(2 * b + r, levels, stride=2 * blocks), :]
+
+
+def join_body(kept, swapped_in, *out):
+    place = lax.axis_index("lev")
+    chip, core = lax.shift_right_logical(place, 1), lax.rem(place, 2)
+    for q in range(4):
+        target = lax.bitwise_xor(chip, q)
+        out[q][core] = kept[target]
+        out[q][1 - core] = swapped_in[target]
 
 
 def reach(first, last, levels):
@@ -133,9 +152,19 @@
     return max(0, math.floor(low) - 1), min(levels, math.ceil(high) + 1)
 
 
-def column_body(sources, per, bands, got, powers, daylight, out_h, thick_s, low_s, top_s, adv_s, pad_s, out, sems):
+def column_body(sources, per, bands, own, beside, low2, high2, low3, high3, powers, daylight, out_h, got, thick_s, low_s, top_s, adv_s, pad_s, out, sems):
     levels = sources * per
     cols = LANES
+    chip = lax.shift_right_logical(lax.axis_index("lev"), 1)
+
+    def place(pieces):
+        for q, piece in enumerate(pieces):
+            source = lax.bitwise_xor(chip, q)
+            for c in range(2):
+                got[2 * source + c] = piece[c]
+
+    pl.when(chip < 2)(lambda: place((own, beside, low2, low3)))
+    pl.when(chip >= 2)(lambda: place((own, beside, high2, high3)))
     for r in range(2):
         for s in range(sources):
             for f in range(3):
@@ -221,6 +250,15 @@
     return lax.ppermute(x, axis, [way for i, j in pairs for way in ((i, j), (j, i))])
 
 
+def core_swap(x):
+    size = lax.axis_size("lev")
+    return lax.ppermute(x, "lev", [(i, i ^ 1) for i in range(size)])
+
+
+def between_chips(x, pairs):
+    return lax.ppermute(x, "lev", [(2 * a + c, 2 * b + c) for a, b in pairs for c in range(2)])
+
+
 def local(fields, north, south, east, limiter, thickness, sunlit, absorb, solar_flux):
     _, levels, _, cols = fields.shape
     blocks = cols // LANES
@@ -252,22 +290,37 @@
         cost_estimate=pl.CostEstimate(flops=100000, bytes_accessed=1000000, transcendentals=0),
         name="prepare",
     )(sunlit.reshape(-1), absorb, solar_flux)
-    pieces = pl.pallas_call(
+    half = jax.ShapeDtypeStruct((sources // 2, 8 * levels, LANES), jnp.float32)
+    kept, given_away = pl.pallas_call(
         lambda *refs: advect_body(levels, blocks, *refs),
-        out_shape=jax.ShapeDtypeStruct((blocks, 8 * levels, LANES), jnp.float32),
+        out_shape=(half, half),
         in_specs=[vmem] * 10,
-        out_specs=vmem,
+        out_specs=(vmem, vmem),
         compiler_params=params,
         name="advect",
     )(*held, near, far, powers, daylight)
-    got = lax.all_to_all(pieces, "lev", 0, 0)
+    pair = jax.ShapeDtypeStruct((2, 8 * levels, LANES), jnp.float32)
+    own, beside, second, third = pl.pallas_call(
+        join_body,
+        out_shape=[pair] * 4,
+        in_specs=[vmem] * 2,
+        out_specs=[vmem] * 4,
+        compiler_params=params,
+        name="join",
+    )(kept, core_swap(given_away))
+    beside = between_chips(beside, ((0, 1), (1, 0), (2, 3), (3, 2)))
+    low3 = between_chips(third, ((2, 1), (3, 0)))
+    low2 = between_chips(second, ((2, 0), (3, 1)))
+    high3 = between_chips(third, ((0, 3), (1, 2)))
+    high2 = between_chips(second, ((0, 2), (1, 3)))
     whole = sources * levels
     result = pl.pallas_call(
         lambda *refs: column_body(sources, levels, bands, *refs),
         out_shape=jax.ShapeDtypeStruct((3, whole * 2, LANES), jnp.float32),
-        in_specs=[vmem] * 3,
+        in_specs=[vmem] * 8,
         out_specs=hbm,
         scratch_shapes=[
+            pltpu.VMEM((sources, 8 * levels, LANES), jnp.float32),
             pltpu.VMEM((2, whole, LANES), jnp.float32),
             pltpu.VMEM((2, whole, LANES), jnp.float32),
             pltpu.VMEM((2, whole, LANES), jnp.float32),
@@ -278,7 +331,7 @@
         ],
         compiler_params=params,
         name="column",
-    )(got, powers, daylight)
+    )(own, beside, low2, high2, low3, high3, powers, daylight)
     return result.reshape(3, whole, 2, LANES)
 
 
@@ -295,4 +348,5 @@
         P(),
     )
     out_specs = P(None, None, "lat", "lev")
+
     return jax.shard_map(local, mesh=mesh, in_specs=in_specs, out_specs=out_specs, check_vma=False)

time: 63 us -> 73.9 us (1.17)
  the two profiles are of different devices: /device:TPU:56 before, /device:TPU:6 now
where the time goes in v3:
time: 73.9 us; the launch traced here: 73.6 us
  starting transfers between devices  50.3 us (68%)
  waiting for transfers between devices  17.9 us (24%)
  Pallas kernels  5.19 us (7%)
    ppermute x5, starting transfers between devices, between_chips(): lax.ppermute(x, 'lev', [(2 * a + c, 2 * b + c) for a, b in pairs for c in...  35.2 us
    ppermute x2, starting transfers between devices, swapped(): lax.ppermute(x, axis, [way for i, j in pairs for way in ((i, j), (j, i))])  13.1 us
    ppermute x5, waiting for transfers between devices, between_chips(): lax.ppermute(x, 'lev', [(2 * a + c, 2 * b + c) for a, b in pairs for c in...  8.8 us
    ppermute x2, waiting for transfers between devices, swapped(): lax.ppermute(x, axis, [way for i, j in pairs for way in ((i, j), (j, i))])  7.81 us
    pallas_call x1, Pallas kernels, local(): pl.pallas_call(lambda *refs: column_body(sources, levels, bands, *refs),...  2.91 us
    ppermute x1, starting transfers between devices, core_swap(): return lax.ppermute(x, 'lev', [(i, i ^ 1) for i in range(size)])  1.92 us
  transfers between devices with their start and end apart: 8, of which 4 were waited for; matrix products, arithmetic and copies ran while one was open for 0% of the time, Pallas kernels for 1%

profile of v3, /device:TPU:6, one launch (start us, length us, event | category | flops | bytes accessed | tf_op | source)
XLA Modules:
  0.0 73.6 jit_solution(5229563330684622689)
XLA Ops:
  0.0 1.2 %pack.1 = (f32[7,8,1024]{2,1,0:T(8,128)S(1)}, f32[7,8,1024]{2,1,0:T(8,128)S(1)}, f32[3,128,128]{2,1,0:T(8,128)S(1)}, f32[128,128]{1,0:T(8,128)S(1)}, f32[128,128...) custom-call(f32[3,128,128]{2,1,0:T(8,128)} %bitcast.33, ...), custom_call_target="tpu_custom_call" | custom-call | tf_op jit(solution)/shard_map/pack/pallas_call | solution.py:273
  1.2 4.3 %collective-permute-start = (f32[7,8,1024]{2,1,0:T(8,128)S(1)}, f32[7,8,1024]{2,1,0:T(8,128)S(1)}, u32[]{:S(2)}, u32[]{:S(2)}) collective-permute-start(f32[7,8,1024]{2,1,0:T(8,128)S(1)} %get-tuple-element.27), channel_id=1, source_target_pairs={{0,8},{8,0},{16,24},{24,16},{32,40},{40,32},{48,56},{56,48},{64,72... | collective-permute-start | bytes 688136 | tf_op jit(solution)/shard_map/ppermute | solution.py:250
  5.5 0.0 copy-start.2
  5.5 0.0 copy-start
  5.5 0.0 copy-start.1
  5.5 8.8 %collective-permute-start.1 = (f32[7,8,1024]{2,1,0:T(8,128)S(1)}, f32[7,8,1024]{2,1,0:T(8,128)S(1)}, u32[]{:S(2)}, u32[]{:S(2)}) collective-permute-start(f32[7,8,1024]{2,1,0:T(8,128)S(1)} %get-tuple-element.28), channel_id=1, source_target_pairs={{8,16},{16,8},{24,32},{32,24},{40,48},{48,40},{56,64},{64,56},{72,... | collective-permute-start | bytes 688136 | tf_op jit(solution)/shard_map/ppermute | solution.py:250
  14.4 0.0 copy-done.2
  14.4 0.0 copy-done
  14.4 0.0 copy-done.1
  14.4 0.7 prepare.1
  15.1 0.0 collective-permute-done.refs_6_
  15.1 7.8 %collective-permute-done.1.refs_7_ = f32[7,8,1024]{2,1,0:T(8,128)S(1)} collective-permute-done((f32[7,8,1024]{2,1,0:T(8,128)S(1)}, f32[7,8,1024]{2,1,0:T(8,128)S(1)}, u32[]{:S(2)}, u32[]{:S(2)}) %collective-permute-start.1) | collective-permute-done | bytes 229408 | tf_op jit(solution)/shard_map/ppermute | solution.py:250
  22.9 0.4 advect.1
  23.3 1.9 %collective-permute-start.2 = (f32[4,64,128]{2,1,0:T(8,128)S(1)}, f32[4,64,128]{2,1,0:T(8,128)S(1)}, u32[]{:S(2)}, u32[]{:S(2)}) collective-permute-start(f32[4,64,128]{2,1,0:T(8,128)S(1)} %get-tuple-element.32), channel_id=1, source_target_pairs={{0,1},{1,0},{2,3},{3,2},{4,5},{5,4},{6,7},{7,6},{8,9},{9,8},{10,11... | collective-permute-start | bytes 393224 | tf_op jit(solution)/shard_map/ppermute | solution.py:255
  25.2 1.3 %collective-permute-done.2.swapped_in = f32[4,64,128]{2,1,0:T(8,128)S(1)} collective-permute-done((f32[4,64,128]{2,1,0:T(8,128)S(1)}, f32[4,64,128]{2,1,0:T(8,128)S(1)}, u32[]{:S(2)}, u32[]{:S(2)}) %collective-permute-start.2) | collective-permute-done | bytes 131104 | tf_op jit(solution)/shard_map/ppermute | solution.py:255
  26.6 10.9 %collective-permute-start.3 = (f32[2,64,128]{2,1,0:T(8,128)S(1)}, f32[2,64,128]{2,1,0:T(8,128)S(1)}, u32[]{:S(2)}, u32[]{:S(2)}) collective-permute-start(f32[2,64,128]{2,1,0:T(8,128)S(1)} %get-tuple-element.34), channel_id=1, source_target_pairs={{0,2},{1,3},{2,0},{3,1},{4,6},{5,7},{6,4},{7,5},{8,10},{9,11},{10,... | collective-permute-start | bytes 196616 | tf_op jit(solution)/shard_map/ppermute | solution.py:259
  37.5 12.1 %collective-permute-start.5 = (f32[2,64,128]{2,1,0:T(8,128)S(1)}, f32[2,64,128]{2,1,0:T(8,128)S(1)}, u32[]{:S(2)}, u32[]{:S(2)}) collective-permute-start(f32[2,64,128]{2,1,0:T(8,128)S(1)} %get-tuple-element.35), channel_id=1, source_target_pairs={{0,4},{1,5},{2,6},{3,7},{8,12},{9,13},{10,14},{11,15},{16,20},{17,... | collective-permute-start | bytes 196616 | tf_op jit(solution)/shard_map/ppermute | solution.py:259
  49.6 1.3 %collective-permute-start.4 = (f32[2,64,128]{2,1,0:T(8,128)S(1)}, f32[2,64,128]{2,1,0:T(8,128)S(1)}, u32[]{:S(2)}, u32[]{:S(2)}) collective-permute-start(f32[2,64,128]{2,1,0:T(8,128)S(1)} %get-tuple-element.35), channel_id=1, source_target_pairs={{4,0},{5,1},{6,2},{7,3},{12,8},{13,9},{14,10},{15,11},{20,16},{21,... | collective-permute-start | bytes 196616 | tf_op jit(solution)/shard_map/ppermute | solution.py:259
  50.9 9.6 %collective-permute-start.7 = (f32[2,64,128]{2,1,0:T(8,128)S(1)}, f32[2,64,128]{2,1,0:T(8,128)S(1)}, u32[]{:S(2)}, u32[]{:S(2)}) collective-permute-start(f32[2,64,128]{2,1,0:T(8,128)S(1)} %get-tuple-element.36), channel_id=1, source_target_pairs={{0,6},{1,7},{2,4},{3,5},{8,14},{9,15},{10,12},{11,13},{16,22},{17,... | collective-permute-start | bytes 196616 | tf_op jit(solution)/shard_map/ppermute | solution.py:259
  60.6 1.3 %collective-permute-start.6 = (f32[2,64,128]{2,1,0:T(8,128)S(1)}, f32[2,64,128]{2,1,0:T(8,128)S(1)}, u32[]{:S(2)}, u32[]{:S(2)}) collective-permute-start(f32[2,64,128]{2,1,0:T(8,128)S(1)} %get-tuple-element.36), channel_id=1, source_target_pairs={{4,2},{5,3},{6,0},{7,1},{12,10},{13,11},{14,8},{15,9},{20,18},{21,... | collective-permute-start | bytes 196616 | tf_op jit(solution)/shard_map/ppermute | solution.py:259
  61.9 0.0 collective-permute-done.3.refs_1_
  61.9 0.0 collective-permute-done.5.refs_3_
  61.9 2.7 %collective-permute-done.4.refs_2_ = f32[2,64,128]{2,1,0:T(8,128)S(1)} collective-permute-done((f32[2,64,128]{2,1,0:T(8,128)S(1)}, f32[2,64,128]{2,1,0:T(8,128)S(1)}, u32[]{:S(2)}, u32[]{:S(2)}) %collective-permute-start.4) | collective-permute-done | bytes 65568 | tf_op jit(solution)/shard_map/ppermute | solution.py:259
  64.5 0.0 collective-permute-done.7.refs_5_
  64.5 6.1 %collective-permute-done.6.refs_4_ = f32[2,64,128]{2,1,0:T(8,128)S(1)} collective-permute-done((f32[2,64,128]{2,1,0:T(8,128)S(1)}, f32[2,64,128]{2,1,0:T(8,128)S(1)}, u32[]{:S(2)}, u32[]{:S(2)}) %collective-permute-start.6) | collective-permute-done | bytes 65568 | tf_op jit(solution)/shard_map/ppermute | solution.py:259
  70.7 2.9 %column.1 = f32[3,128,128]{2,1,0:T(8,128)} custom-call(f32[2,64,128]{2,1,0:T(8,128)S(1)} %get-tuple-element.33.refs_0_, f32[2,64,128]{2,1,0:T(8,128)S(1)} %collective-permute-done.3.refs_1_, f32[2,64,128]{2,1,0:T(8,128)S(1)} %collective-permute-done.4.refs_2_, f32[2,64,128]{2,1,0:T(8,128)S(1)} %collective-permute-done.5.refs_3_, ...), custom_call_target="tpu_custom_call" | custom-call | tf_op jit(solution)/shard_map/column/pallas_call | solution.py:317
  (1 shorter events, 0.0 us)
Async XLA Ops:
  1.2 13.9 %collective-permute-start = (f32[7,8,1024]{2,1,0:T(8,128)S(1)}, f32[7,8,1024]{2,1,0:T(8,128)S(1)}, u32[]{:S(2)}, u32[]{:S(2)}) collective-permute-start(f32[7,8,1024]{2,1,0:T(8,128)S(1)} %get-tuple-element.27), channel_id=1, source_target_pairs={{0,8},{8,0},{16,24},{24,16},{32,40},{40,32},{48,56},{56,48},{64,72... | collective-permute-start | bytes 688136 | tf_op jit(solution)/shard_map/ppermute | solution.py:250
  5.5 8.9 %copy-start.2 = (f32[64]{0:T(128)S(1)}, f32[64]{0:T(128)}, u32[]{:S(2)}) copy-start(f32[64]{0:T(128)} %refs_2_.1) | copy-start | bytes 772
  5.5 8.9 %copy-start = (f32[2,64]{1,0:T(2,128)S(1)}, f32[2,64]{1,0:T(2,128)}, u32[]{:S(2)}) copy-start(f32[2,64]{1,0:T(2,128)} %refs_1_.1) | copy-start | bytes 1540
  5.5 8.9 %copy-start.1 = (s32[2,1]{0,1:T(1,128)S(1)}, s32[2,1]{0,1:T(1,128)}, u32[]{:S(2)}) copy-start(s32[2,1]{0,1:T(1,128)} %param.15) | copy-start | bytes 28
  5.5 17.4 %collective-permute-start.1 = (f32[7,8,1024]{2,1,0:T(8,128)S(1)}, f32[7,8,1024]{2,1,0:T(8,128)S(1)}, u32[]{:S(2)}, u32[]{:S(2)}) collective-permute-start(f32[7,8,1024]{2,1,0:T(8,128)S(1)} %get-tuple-element.28), channel_id=1, source_target_pairs={{8,16},{16,8},{24,32},{32,24},{40,48},{48,40},{56,64},{64,56},{72,... | collective-permute-start | bytes 688136 | tf_op jit(solution)/shard_map/ppermute | solution.py:250
  23.3 3.2 %collective-permute-start.2 = (f32[4,64,128]{2,1,0:T(8,128)S(1)}, f32[4,64,128]{2,1,0:T(8,128)S(1)}, u32[]{:S(2)}, u32[]{:S(2)}) collective-permute-start(f32[4,64,128]{2,1,0:T(8,128)S(1)} %get-tuple-element.32), channel_id=1, source_target_pairs={{0,1},{1,0},{2,3},{3,2},{4,5},{5,4},{6,7},{7,6},{8,9},{9,8},{10,11... | collective-permute-start | bytes 393224 | tf_op jit(solution)/shard_map/ppermute | solution.py:255
  26.6 35.3 %collective-permute-start.3 = (f32[2,64,128]{2,1,0:T(8,128)S(1)}, f32[2,64,128]{2,1,0:T(8,128)S(1)}, u32[]{:S(2)}, u32[]{:S(2)}) collective-permute-start(f32[2,64,128]{2,1,0:T(8,128)S(1)} %get-tuple-element.34), channel_id=1, source_target_pairs={{0,2},{1,3},{2,0},{3,1},{4,6},{5,7},{6,4},{7,5},{8,10},{9,11},{10,... | collective-permute-start | bytes 196616 | tf_op jit(solution)/shard_map/ppermute | solution.py:259
  37.5 24.4 %collective-permute-start.5 = (f32[2,64,128]{2,1,0:T(8,128)S(1)}, f32[2,64,128]{2,1,0:T(8,128)S(1)}, u32[]{:S(2)}, u32[]{:S(2)}) collective-permute-start(f32[2,64,128]{2,1,0:T(8,128)S(1)} %get-tuple-element.35), channel_id=1, source_target_pairs={{0,4},{1,5},{2,6},{3,7},{8,12},{9,13},{10,14},{11,15},{16,20},{17,... | collective-permute-start | bytes 196616 | tf_op jit(solution)/shard_map/ppermute | solution.py:259
  49.6 14.9 %collective-permute-start.4 = (f32[2,64,128]{2,1,0:T(8,128)S(1)}, f32[2,64,128]{2,1,0:T(8,128)S(1)}, u32[]{:S(2)}, u32[]{:S(2)}) collective-permute-start(f32[2,64,128]{2,1,0:T(8,128)S(1)} %get-tuple-element.35), channel_id=1, source_target_pairs={{4,0},{5,1},{6,2},{7,3},{12,8},{13,9},{14,10},{15,11},{20,16},{21,... | collective-permute-start | bytes 196616 | tf_op jit(solution)/shard_map/ppermute | solution.py:259
  50.9 13.6 %collective-permute-start.7 = (f32[2,64,128]{2,1,0:T(8,128)S(1)}, f32[2,64,128]{2,1,0:T(8,128)S(1)}, u32[]{:S(2)}, u32[]{:S(2)}) collective-permute-start(f32[2,64,128]{2,1,0:T(8,128)S(1)} %get-tuple-element.36), channel_id=1, source_target_pairs={{0,6},{1,7},{2,4},{3,5},{8,14},{9,15},{10,12},{11,13},{16,22},{17,... | collective-permute-start | bytes 196616 | tf_op jit(solution)/shard_map/ppermute | solution.py:259
  60.6 10.1 %collective-permute-start.6 = (f32[2,64,128]{2,1,0:T(8,128)S(1)}, f32[2,64,128]{2,1,0:T(8,128)S(1)}, u32[]{:S(2)}, u32[]{:S(2)}) collective-permute-start(f32[2,64,128]{2,1,0:T(8,128)S(1)} %get-tuple-element.36), channel_id=1, source_target_pairs={{4,2},{5,3},{6,0},{7,1},{12,10},{13,11},{14,8},{15,9},{20,18},{21,... | collective-permute-start | bytes 196616 | tf_op jit(solution)/shard_map/ppermute | solution.py:259

commit v4 on v3

--- a/solution.py
+++ b/solution.py
@@ -37,7 +37,8 @@
 
 
 def pack_body(levels, blocks, *refs):
-    sources, near, far, held, sems = refs[:6], refs[6], refs[7], refs[8:14], refs[14]
+    sources, near, far, held, sems = refs[:6], refs[6:8], refs[8:10], refs[10:16], refs[16]
+    half = blocks * LANES // 2
     copies = [pltpu.make_async_copy(src, dst, sems.at[i]) for i, (src, dst) in enumerate(zip(sources, held))]
     for copy in copies:
         copy.start()
@@ -45,23 +46,27 @@
         copy.wait()
     fields, north, south, limiter = held[:4]
 
+    def put(halves, at, value):
+        halves[0][at] = value[:, :half]
+        halves[1][at] = value[:, half:]
+
     def pack(up, down):
         nc = row_of(north, 1, levels, blocks)
         wb, wf = slope_weights(row_of(limiter, 1, levels, blocks))
         gain = nc * (0.5 * (1.0 - nc))
-        up[6] = gain * wf
+        put(up, 6, gain * wf)
         sc = row_of(south, 0, levels, blocks)
         vb, vf = slope_weights(row_of(limiter, 0, levels, blocks))
         loss = sc * (0.5 * (1.0 - sc))
-        down[6] = loss * vb
+        put(down, 6, loss * vb)
         for f in range(3):
             low = row_of(fields, 0, levels, blocks, (f,))
             top = row_of(fields, 1, levels, blocks, (f,))
             step = top - low
-            up[f] = top
-            up[3 + f] = nc * top + gain * (wb * step - wf * top)
-            down[f] = low
-            down[3 + f] = sc * low - loss * (vb * low + vf * step)
+            put(up, f, top)
+            put(up, 3 + f, nc * top + gain * (wb * step - wf * top))
+            put(down, f, low)
+            put(down, 3 + f, sc * low - loss * (vb * low + vf * step))
 
     odd = lax.rem(lax.axis_index("lat"), 2) == 1
     pl.when(jnp.logical_not(odd))(lambda: pack(near, far))
@@ -79,14 +84,16 @@
         daylight[r] = jnp.full((8, LANES), lit[r].astype(jnp.float32), jnp.float32)
 
 
-def advect_body(levels, blocks, *refs):
+def advect_body(levels, blocks, part, *refs):
     core = lax.rem(lax.axis_index("lev"), 2)
-    pl.when(core == 0)(lambda: advect(levels, blocks, *refs[:8], refs[10], refs[11]))
-    pl.when(core == 1)(lambda: advect(levels, blocks, *refs[:8], refs[11], refs[10]))
-
-
-def advect(levels, blocks, fields, north, south, limiter, east, thick, near, far, even, odd):
+    pl.when(core == 0)(lambda: advect(levels, blocks, part, *refs[:8], refs[-2], refs[-1]))
+    pl.when(core == 1)(lambda: advect(levels, blocks, part, *refs[:8], refs[-1], refs[-2]))
+
+
+def advect(levels, blocks, part, fields, north, south, limiter, east, thick, near, far, even, odd):
     above_far = lax.rem(lax.axis_index("lat"), 2) == 1
+    cols = blocks * LANES
+    first_block = part * (blocks // 2)
 
     def below(i):
         return jnp.where(above_far, near[i], far[i])
@@ -94,54 +101,52 @@
     def above(i):
         return jnp.where(above_far, far[i], near[i])
 
-    cols = blocks * LANES
-    weights, rise_gain, sink_gain, ncs, scs = [], [], [], [], []
+    def cut(value):
+        return value[:, part * (cols // 2) : (part + 1) * (cols // 2)]
+
+    weights, ncs, scs, ecs = [], [], [], []
     for r in range(2):
         weights.append(slope_weights(row_of(limiter, r, levels, blocks)))
-        nc = row_of(north, r, levels, blocks)
-        sc = row_of(south, r, levels, blocks)
-        ncs.append(nc)
-        scs.append(sc)
-        rise_gain.append(nc * (0.5 * (1.0 - nc)))
-        sink_gain.append(sc * (0.5 * (1.0 - sc)))
-    ecs = [row_of(east, r, levels, blocks) for r in range(2)]
+        ncs.append(cut(row_of(north, r, levels, blocks)))
+        scs.append(cut(row_of(south, r, levels, blocks)))
+        ecs.append(row_of(east, r, levels, blocks))
+    rise_gain = [nc * (0.5 * (1.0 - nc)) for nc in ncs]
+    sink_gain = [sc * (0.5 * (1.0 - sc)) for sc in scs]
     east_gain = [ec * (0.5 * (1.0 - ec)) for ec in ecs]
     for f in range(3):
-        rows = [row_of(fields, r, levels, blocks, (f,)) for r in range(2)]
-        before = below(f)
-        after = above(f)
-        diffs = [rows[0] - before, rows[1] - rows[0], after - rows[1]]
+        whole = [row_of(fields, r, levels, blocks, (f,)) for r in range(2)]
+        rows = [cut(row) for row in whole]
+        diffs = [rows[0] - below(f), rows[1] - rows[0], above(f) - rows[1]]
         rise, sink, kept = [], [], []
         for r in range(2):
             wb, wf = weights[r]
-            slope = wb * diffs[r] + wf * diffs[r + 1]
+            slope = cut(wb) * diffs[r] + cut(wf) * diffs[r + 1]
             rise.append(ncs[r] * rows[r] + rise_gain[r] * slope)
             sink.append(scs[r] * rows[r] - sink_gain[r] * slope)
-            step = rows[r] - pltpu.roll(rows[r], 1, 1)
+            step = whole[r] - pltpu.roll(whole[r], 1, 1)
             zonal = wb * step + wf * pltpu.roll(step, cols - 1, 1)
-            going = ecs[r] * rows[r] + east_gain[r] * zonal
-            kept.append(rows[r] - (going - pltpu.roll(going, 1, 1)))
+            going = ecs[r] * whole[r] + east_gain[r] * zonal
+            kept.append(rows[r] - cut(going - pltpu.roll(going, 1, 1)))
         from_below = below(3 + f) + below(6) * rows[0]
         from_above = above(3 + f) + above(6) * rows[1]
         first = kept[0] - (rise[0] + sink[0]) + (from_below + sink[1])
         second = kept[1] - (rise[1] + sink[1]) + (rise[0] + from_above)
         for r, value in enumerate((first, second)):
-            for b in range(blocks):
-                out = (even, odd)[b % 2]
-                out[b // 2, pl.ds((r * 4 + f) * levels, levels), :] = value[:, b * LANES : (b + 1) * LANES]
-    for r in range(2):
-        for b in range(blocks):
-            out = (even, odd)[b % 2]
-            out[b // 2, pl.ds((r * 4 + 3) * levels, levels), :] = thick[pl.ds(2 * b + r, levels, stride=2 * blocks), :]
-
-
-def join_body(kept, swapped_in, *out):
+            for b in range(blocks // 2):
+                (even, odd)[b % 2][b // 2, pl.ds((r * 4 + f) * levels, levels), :] = value[:, b * LANES : (b + 1) * LANES]
+    for r in range(2):
+        for b in range(blocks // 2):
+            (even, odd)[b % 2][b // 2, pl.ds((r * 4 + 3) * levels, levels), :] = thick[
+                pl.ds(2 * (first_block + b) + r, levels, stride=2 * blocks), :
+            ]
+
+
+def join_body(kept, swapped_in, across, straight):
     place = lax.axis_index("lev")
-    chip, core = lax.shift_right_logical(place, 1), lax.rem(place, 2)
-    for q in range(4):
-        target = lax.bitwise_xor(chip, q)
-        out[q][core] = kept[target]
-        out[q][1 - core] = swapped_in[target]
+    core, parity = lax.rem(place, 2), lax.rem(lax.shift_right_logical(place, 1), 2)
+    for out, target in ((across, 1 - parity), (straight, parity)):
+        out[core] = kept[target]
+        out[1 - core] = swapped_in[target]
 
 
 def reach(first, last, levels):
@@ -152,7 +157,7 @@
     return max(0, math.floor(low) - 1), min(levels, math.ceil(high) + 1)
 
 
-def column_body(sources, per, bands, own, beside, low2, high2, low3, high3, powers, daylight, out_h, got, thick_s, low_s, top_s, adv_s, pad_s, out, sems):
+def column_body(sources, per, bands, own1, beside1, second1, third1, own2, beside2, second2, third2, powers, daylight, out_h, got, low_s, top_s, pad_s, out, sems):
     levels = sources * per
     cols = LANES
     chip = lax.shift_right_logical(lax.axis_index("lev"), 1)
@@ -163,21 +168,31 @@
             for c in range(2):
                 got[2 * source + c] = piece[c]
 
-    pl.when(chip < 2)(lambda: place((own, beside, low2, low3)))
-    pl.when(chip >= 2)(lambda: place((own, beside, high2, high3)))
-    for r in range(2):
-        for s in range(sources):
-            for f in range(3):
-                adv_s[r, f, pl.ds(s * per, per), :] = got[s, pl.ds((r * 4 + f) * per, per), :]
-            thick_s[r, pl.ds(s * per, per), :] = got[s, pl.ds((r * 4 + 3) * per, per), :]
+    pl.when(chip < 2)(lambda: place((own1, beside1, second1, third1)))
+    pl.when(chip >= 2)(lambda: place((own2, beside2, second2, third2)))
     at_row = lax.broadcasted_iota(jnp.int32, (levels, levels), 0)
     at_col = lax.broadcasted_iota(jnp.int32, (levels, levels), 1)
-    triangle = jnp.where(at_row >= at_col, 1.0, 0.0).astype(jnp.float32)
+    triangle = jnp.where(at_row >= at_col, 1.0, 0.0).astype(jnp.bfloat16)
 
     def running(x):
-        return jnp.dot(triangle, x, precision=lax.Precision.HIGHEST, preferred_element_type=jnp.float32)
-
-    thick = jnp.concatenate([thick_s[0], thick_s[1]], axis=1)
+        total = None
+        for _ in range(3):
+            part = x.astype(jnp.bfloat16)
+            x = x - part.astype(jnp.float32)
+            sums = jnp.dot(triangle, part, preferred_element_type=jnp.float32)
+            total = sums if total is None else total + sums
+        return total
+
+    def piece(s, r, f):
+        return got[s, pl.ds((r * 4 + f) * per, per), :]
+
+    def level(j, r, f):
+        line = got[j // per, pl.ds((r * 4 + f) * per + j % per, 1), :]
+        return jnp.broadcast_to(line, (8, cols))
+
+    thick = jnp.concatenate(
+        [jnp.concatenate([piece(s, r, 3) for s in range(sources)], axis=0) for r in range(2)], axis=1
+    )
     top = running(thick)
     low = top - thick
     step = 8
@@ -203,7 +218,7 @@
                 edge_low = jnp.broadcast_to(low_s[r, pl.ds(j, 1), :], (step, cols))
                 shared = jnp.maximum(jnp.minimum(edge_top, ceiling) - jnp.maximum(edge_low, bottom), 0.0)
                 for f in range(3):
-                    sums[f] = sums[f] + shared * jnp.broadcast_to(adv_s[r, f, pl.ds(j, 1), :], (step, cols))
+                    sums[f] = sums[f] + shared * level(j, r, f)
             values = [total * inv8 for total in sums]
             pad_s[r, pl.ds(step + k, step), :] = values[0]
             out[1, pl.ds(2 * k + r, step, stride=2), :] = values[1]
@@ -269,18 +284,20 @@
     hbm = pl.BlockSpec(memory_space=pltpu.HBM)
     params = pltpu.CompilerParams(vmem_limit_bytes=kernel_vmem)
     given = [pltpu.with_memory_space_constraint(block_rows(x), pltpu.HBM) for x in (fields, north, south, limiter, east, thickness)]
-    halo = jax.ShapeDtypeStruct((7, levels, cols), jnp.float32)
-    near, far, *held = pl.pallas_call(
+    halo = jax.ShapeDtypeStruct((7, levels, cols // 2), jnp.float32)
+    near1, near2, far1, far2, *held = pl.pallas_call(
         lambda *refs: pack_body(levels, blocks, *refs),
-        out_shape=[halo, halo] + [jax.ShapeDtypeStruct(x.shape, x.dtype) for x in given],
+        out_shape=[halo] * 4 + [jax.ShapeDtypeStruct(x.shape, x.dtype) for x in given],
         in_specs=[hbm] * 6,
-        out_specs=[vmem] * 8,
+        out_specs=[vmem] * 10,
         scratch_shapes=[pltpu.SemaphoreType.DMA((6,))],
         compiler_params=params,
         name="pack",
     )(*given)
-    far = swapped(far, "lat", 1)
-    near = swapped(near, "lat", 0)
+    far1 = swapped(far1, "lat", 1)
+    near1 = swapped(near1, "lat", 0)
+    far2 = swapped(far2, "lat", 1)
+    near2 = swapped(near2, "lat", 0)
     powers, daylight = pl.pallas_call(
         lambda *refs: prepare_body(bands, *refs),
         out_shape=(jax.ShapeDtypeStruct((3 * bands, LANES), jnp.float32), jax.ShapeDtypeStruct((2, 8, LANES), jnp.float32)),
@@ -290,48 +307,46 @@
         cost_estimate=pl.CostEstimate(flops=100000, bytes_accessed=1000000, transcendentals=0),
         name="prepare",
     )(sunlit.reshape(-1), absorb, solar_flux)
-    half = jax.ShapeDtypeStruct((sources // 2, 8 * levels, LANES), jnp.float32)
-    kept, given_away = pl.pallas_call(
-        lambda *refs: advect_body(levels, blocks, *refs),
-        out_shape=(half, half),
-        in_specs=[vmem] * 10,
-        out_specs=(vmem, vmem),
-        compiler_params=params,
-        name="advect",
-    )(*held, near, far, powers, daylight)
     pair = jax.ShapeDtypeStruct((2, 8 * levels, LANES), jnp.float32)
-    own, beside, second, third = pl.pallas_call(
-        join_body,
-        out_shape=[pair] * 4,
-        in_specs=[vmem] * 2,
-        out_specs=[vmem] * 4,
-        compiler_params=params,
-        name="join",
-    )(kept, core_swap(given_away))
-    beside = between_chips(beside, ((0, 1), (1, 0), (2, 3), (3, 2)))
-    low3 = between_chips(third, ((2, 1), (3, 0)))
-    low2 = between_chips(second, ((2, 0), (3, 1)))
-    high3 = between_chips(third, ((0, 3), (1, 2)))
-    high2 = between_chips(second, ((0, 2), (1, 3)))
+
+    def advected(part, near, far, *after):
+        kept, given_away = pl.pallas_call(
+            lambda *refs: advect_body(levels, blocks, part, *refs),
+            out_shape=(pair, pair),
+            in_specs=[vmem] * (8 + len(after)),
+            out_specs=(vmem, vmem),
+            compiler_params=params,
+        )(*held, near, far, *after)
+        swapped_in = core_swap(given_away)
+        return pl.pallas_call(
+            join_body, out_shape=(pair, pair), in_specs=[vmem] * 2, out_specs=(vmem, vmem), compiler_params=params
+        )(kept, swapped_in)
+
+    across1, straight1 = advected(0, near1, far1, powers, daylight)
+    third1 = between_chips(across1, ((2, 1), (3, 0)))
+    second1 = between_chips(straight1, ((2, 0), (3, 1)))
+    beside1 = between_chips(across1, ((0, 1), (1, 0)))
+    across2, straight2 = advected(1, near2, far2)
+    beside2 = between_chips(across2, ((2, 3), (3, 2)))
+    third2 = between_chips(across2, ((0, 3), (1, 2)))
+    second2 = between_chips(straight2, ((0, 2), (1, 3)))
     whole = sources * levels
     result = pl.pallas_call(
         lambda *refs: column_body(sources, levels, bands, *refs),
         out_shape=jax.ShapeDtypeStruct((3, whole * 2, LANES), jnp.float32),
-        in_specs=[vmem] * 8,
+        in_specs=[vmem] * 10,
         out_specs=hbm,
         scratch_shapes=[
             pltpu.VMEM((sources, 8 * levels, LANES), jnp.float32),
             pltpu.VMEM((2, whole, LANES), jnp.float32),
             pltpu.VMEM((2, whole, LANES), jnp.float32),
-            pltpu.VMEM((2, whole, LANES), jnp.float32),
-            pltpu.VMEM((2, 3, whole, LANES), jnp.float32),
             pltpu.VMEM((2, whole + 16, LANES), jnp.float32),
             pltpu.VMEM((3, whole * 2, LANES), jnp.float32),
             pltpu.SemaphoreType.DMA((3,)),
         ],
         compiler_params=params,
         name="column",
-    )(own, beside, low2, high2, low3, high3, powers, daylight)
+    )(straight1, beside1, second1, third1, straight2, beside2, second2, third2, powers, daylight)
     return result.reshape(3, whole, 2, LANES)
 
 

time: 73.9 us -> 62.2 us (0.84)
  waiting for transfers between devices: 17.9 us -> 11.1 us
  starting transfers between devices: 50.3 us -> 45.2 us
    ppermute x5 -> x6, starting transfers between devices: 35.2 us -> 22.4 us  [between_chips(): lax.ppermute(x, 'lev', [(2 * a + c, 2 * b + c) for a, b in pairs for c in...]
    ppermute x2 -> x4, starting transfers between devices: 13.1 us -> 19 us  [swapped(): lax.ppermute(x, axis, [way for i, j in pairs for way in ((i, j), (j, i))])]
    ppermute x2 -> x4, waiting for transfers between devices: 7.81 us -> 4.6 us  [swapped(): lax.ppermute(x, axis, [way for i, j in pairs for way in ((i, j), (j, i))])]
    ppermute x5 -> x6, waiting for transfers between devices: 8.8 us -> 6.48 us  [between_chips(): lax.ppermute(x, 'lev', [(2 * a + c, 2 * b + c) for a, b in pairs for c in...]
    ppermute x1 -> x2, starting transfers between devices: 1.92 us -> 3.84 us  [core_swap(): return lax.ppermute(x, 'lev', [(i, i ^ 1) for i in range(size)])]
    ppermute x1 -> x2, waiting for transfers between devices: 1.31 us -> 0.01 us  [core_swap(): return lax.ppermute(x, 'lev', [(i, i ^ 1) for i in range(size)])]
  transfers between devices with their start and end apart: 8 -> 12, of which waited for: 4 -> 3; matrix products, arithmetic and copies ran while one was open for 0% -> 0% of each run, Pallas kernels for 1% -> 2%
where the time goes in v4:
time: 62.2 us; the launch traced here: 61.8 us
  starting transfers between devices  45.2 us (73%)
  waiting for transfers between devices  11.1 us (18%)
  Pallas kernels  5.18 us (8%)
    ppermute x6, starting transfers between devices, between_chips(): lax.ppermute(x, 'lev', [(2 * a + c, 2 * b + c) for a, b in pairs for c in...  22.4 us
    ppermute x4, starting transfers between devices, swapped(): lax.ppermute(x, axis, [way for i, j in pairs for way in ((i, j), (j, i))])  19 us
    ppermute x6, waiting for transfers between devices, between_chips(): lax.ppermute(x, 'lev', [(2 * a + c, 2 * b + c) for a, b in pairs for c in...  6.48 us
    ppermute x4, waiting for transfers between devices, swapped(): lax.ppermute(x, axis, [way for i, j in pairs for way in ((i, j), (j, i))])  4.6 us
    ppermute x2, starting transfers between devices, core_swap(): return lax.ppermute(x, 'lev', [(i, i ^ 1) for i in range(size)])  3.84 us
    pallas_call x1, Pallas kernels, local(): pl.pallas_call(lambda *refs: column_body(sources, levels, bands, *refs),...  2.69 us
  transfers between devices with their start and end apart: 12, of which 3 were waited for; matrix products, arithmetic and copies ran while one was open for 0% of the time, Pallas kernels for 2%

profile of v4, /device:TPU:6, one launch (start us, length us, event | category | flops | bytes accessed | tf_op | source)
XLA Modules:
  0.0 61.8 jit_solution(14450581370377430003)
XLA Ops:
  0.0 1.2 %pack.1 = (f32[7,8,512]{2,1,0:T(8,128)S(1)}, f32[7,8,512]{2,1,0:T(8,128)S(1)}, f32[7,8,512]{2,1,0:T(8,128)S(1)}, f32[7,8,512]{2,1,0:T(8,128)S(1)}, f32[3,128,128...) custom-call(f32[3,128,128]{2,1,0:T(8,128)} %bitcast.33, ...), custom_call_target="tpu_custom_call" | custom-call | tf_op jit(solution)/shard_map/pack/pallas_call | solution.py:288
  1.2 4.3 %collective-permute-start = (f32[7,8,512]{2,1,0:T(8,128)S(1)}, f32[7,8,512]{2,1,0:T(8,128)S(1)}, u32[]{:S(2)}, u32[]{:S(2)}) collective-permute-start(f32[7,8,512]{2,1,0:T(8,128)S(1)} %get-tuple-element.31), channel_id=1, source_target_pairs={{0,8},{8,0},{16,24},{24,16},{32,40},{40,32},{48,56},{56,48},{64,72... | collective-permute-start | bytes 344072 | tf_op jit(solution)/shard_map/ppermute | solution.py:265
  5.5 8.7 %collective-permute-start.1 = (f32[7,8,512]{2,1,0:T(8,128)S(1)}, f32[7,8,512]{2,1,0:T(8,128)S(1)}, u32[]{:S(2)}, u32[]{:S(2)}) collective-permute-start(f32[7,8,512]{2,1,0:T(8,128)S(1)} %get-tuple-element.32), channel_id=1, source_target_pairs={{8,16},{16,8},{24,32},{32,24},{40,48},{48,40},{56,64},{64,56},{72,... | collective-permute-start | bytes 344072 | tf_op jit(solution)/shard_map/ppermute | solution.py:265
  14.2 1.9 %collective-permute-start.6 = (f32[7,8,512]{2,1,0:T(8,128)S(1)}, f32[7,8,512]{2,1,0:T(8,128)S(1)}, u32[]{:S(2)}, u32[]{:S(2)}) collective-permute-start(f32[7,8,512]{2,1,0:T(8,128)S(1)} %get-tuple-element.39), channel_id=1, source_target_pairs={{0,8},{8,0},{16,24},{24,16},{32,40},{40,32},{48,56},{56,48},{64,72... | collective-permute-start | bytes 344072 | tf_op jit(solution)/shard_map/ppermute | solution.py:265
  16.1 0.0 copy-start.2
  16.2 0.0 copy-start
  16.2 0.0 copy-start.1
  16.2 4.1 %collective-permute-start.7 = (f32[7,8,512]{2,1,0:T(8,128)S(1)}, f32[7,8,512]{2,1,0:T(8,128)S(1)}, u32[]{:S(2)}, u32[]{:S(2)}) collective-permute-start(f32[7,8,512]{2,1,0:T(8,128)S(1)} %get-tuple-element.40), channel_id=1, source_target_pairs={{8,16},{16,8},{24,32},{32,24},{40,48},{48,40},{56,64},{64,56},{72,... | collective-permute-start | bytes 344072 | tf_op jit(solution)/shard_map/ppermute | solution.py:265
  20.2 0.0 copy-done.2
  20.2 0.0 copy-done
  20.3 0.0 copy-done.1
  20.3 0.7 %prepare.1 = (f32[192,128]{1,0:T(8,128)S(1)}, f32[2,8,128]{2,1,0:T(8,128)S(1)}) custom-call(s32[2]{0:T(128)S(1)} %bitcast.32, f32[2,64]{1,0:T(2,128)S(1)} %copy-done, f32[64]{0:T(128)S(1)} %copy-done.2), custom_call_target="tpu_custom_call" | custom-call | flops 100000 | bytes 1000000 | tf_op jit(solution)/shard_map/prepare/pallas_call | solution.py:301
  20.9 0.0 collective-permute-done.refs_6_
  20.9 0.0 collective-permute-done.1.refs_7_
  20.9 0.3 shard_map.91
  21.3 1.9 %collective-permute-start.2 = (f32[2,64,128]{2,1,0:T(8,128)S(1)}, f32[2,64,128]{2,1,0:T(8,128)S(1)}, u32[]{:S(2)}, u32[]{:S(2)}) collective-permute-start(f32[2,64,128]{2,1,0:T(8,128)S(1)} %get-tuple-element.36), channel_id=1, source_target_pairs={{0,1},{1,0},{2,3},{3,2},{4,5},{5,4},{6,7},{7,6},{8,9},{9,8},{10,11... | collective-permute-start | bytes 196616 | tf_op jit(solution)/shard_map/ppermute | solution.py:270
  23.2 0.0 collective-permute-done.6.refs_6_
  23.2 4.6 %collective-permute-done.7.refs_7_ = f32[7,8,512]{2,1,0:T(8,128)S(1)} collective-permute-done((f32[7,8,512]{2,1,0:T(8,128)S(1)}, f32[7,8,512]{2,1,0:T(8,128)S(1)}, u32[]{:S(2)}, u32[]{:S(2)}) %collective-permute-start.7) | collective-permute-done | bytes 114720 | tf_op jit(solution)/shard_map/ppermute | solution.py:265
  27.8 0.3 shard_map.93
  28.1 1.9 %collective-permute-start.8 = (f32[2,64,128]{2,1,0:T(8,128)S(1)}, f32[2,64,128]{2,1,0:T(8,128)S(1)}, u32[]{:S(2)}, u32[]{:S(2)}) collective-permute-start(f32[2,64,128]{2,1,0:T(8,128)S(1)} %get-tuple-element.42), channel_id=1, source_target_pairs={{0,1},{1,0},{2,3},{3,2},{4,5},{5,4},{6,7},{7,6},{8,9},{9,8},{10,11... | collective-permute-start | bytes 196616 | tf_op jit(solution)/shard_map/ppermute | solution.py:270
  30.0 0.0 collective-permute-done.2.swapped_in
  30.1 1.3 %collective-permute-start.4 = (f32[2,64,128]{2,1,0:T(8,128)S(1)}, f32[2,64,128]{2,1,0:T(8,128)S(1)}, u32[]{:S(2)}, u32[]{:S(2)}) collective-permute-start(f32[2,64,128]{2,1,0:T(8,128)S(1)} %get-tuple-element.37.refs_0_), channel_id=1, source_target_pairs={{4,0},{5,1},{6,2},{7,3},{12,8},{13,9},{14,10},{15,11},{20,16},{21,... | collective-permute-start | bytes 196616 | tf_op jit(solution)/shard_map/ppermute | solution.py:274
  31.4 1.3 %collective-permute-start.5 = (f32[2,64,128]{2,1,0:T(8,128)S(1)}, f32[2,64,128]{2,1,0:T(8,128)S(1)}, u32[]{:S(2)}, u32[]{:S(2)}) collective-permute-start(f32[2,64,128]{2,1,0:T(8,128)S(1)} %get-tuple-element.38), channel_id=1, source_target_pairs={{4,2},{5,3},{6,0},{7,1},{12,10},{13,11},{14,8},{15,9},{20,18},{21,... | collective-permute-start | bytes 196616 | tf_op jit(solution)/shard_map/ppermute | solution.py:274
  32.7 10.9 %collective-permute-start.3 = (f32[2,64,128]{2,1,0:T(8,128)S(1)}, f32[2,64,128]{2,1,0:T(8,128)S(1)}, u32[]{:S(2)}, u32[]{:S(2)}) collective-permute-start(f32[2,64,128]{2,1,0:T(8,128)S(1)} %get-tuple-element.38), channel_id=1, source_target_pairs={{0,2},{1,3},{2,0},{3,1},{8,10},{9,11},{10,8},{11,9},{16,18},{17,19... | collective-permute-start | bytes 196616 | tf_op jit(solution)/shard_map/ppermute | solution.py:274
  43.6 0.0 collective-permute-done.8.swapped_in
  43.6 7.0 %collective-permute-start.10 = (f32[2,64,128]{2,1,0:T(8,128)S(1)}, f32[2,64,128]{2,1,0:T(8,128)S(1)}, u32[]{:S(2)}, u32[]{:S(2)}) collective-permute-start(f32[2,64,128]{2,1,0:T(8,128)S(1)} %get-tuple-element.43.refs_4_), channel_id=1, source_target_pairs={{0,4},{1,5},{2,6},{3,7},{8,12},{9,13},{10,14},{11,15},{16,20},{17,... | collective-permute-start | bytes 196616 | tf_op jit(solution)/shard_map/ppermute | solution.py:274
  50.6 1.3 %collective-permute-start.11 = (f32[2,64,128]{2,1,0:T(8,128)S(1)}, f32[2,64,128]{2,1,0:T(8,128)S(1)}, u32[]{:S(2)}, u32[]{:S(2)}) collective-permute-start(f32[2,64,128]{2,1,0:T(8,128)S(1)} %get-tuple-element.44), channel_id=1, source_target_pairs={{0,6},{1,7},{2,4},{3,5},{8,14},{9,15},{10,12},{11,13},{16,22},{17,... | collective-permute-start | bytes 196616 | tf_op jit(solution)/shard_map/ppermute | solution.py:274
  51.9 0.0 collective-permute-done.4.refs_2_
  51.9 0.7 %collective-permute-start.9 = (f32[2,64,128]{2,1,0:T(8,128)S(1)}, f32[2,64,128]{2,1,0:T(8,128)S(1)}, u32[]{:S(2)}, u32[]{:S(2)}) collective-permute-start(f32[2,64,128]{2,1,0:T(8,128)S(1)} %get-tuple-element.44), channel_id=1, source_target_pairs={{4,6},{5,7},{6,4},{7,5},{12,14},{13,15},{14,12},{15,13},{20,22},{2... | collective-permute-start | bytes 196616 | tf_op jit(solution)/shard_map/ppermute | solution.py:274
  52.6 0.0 collective-permute-done.5.refs_3_
  52.6 0.0 collective-permute-done.3.refs_1_
  52.6 0.4 collective-permute-done.10.refs_6_
  53.0 6.0 %collective-permute-done.11.refs_7_ = f32[2,64,128]{2,1,0:T(8,128)S(1)} collective-permute-done((f32[2,64,128]{2,1,0:T(8,128)S(1)}, f32[2,64,128]{2,1,0:T(8,128)S(1)}, u32[]{:S(2)}, u32[]{:S(2)}) %collective-permute-start.11) | collective-permute-done | bytes 65568 | tf_op jit(solution)/shard_map/ppermute | solution.py:274
  59.1 0.0 collective-permute-done.9.refs_5_
  59.1 2.7 %column.1 = f32[3,128,128]{2,1,0:T(8,128)} custom-call(f32[2,64,128]{2,1,0:T(8,128)S(1)} %get-tuple-element.37.refs_0_, f32[2,64,128]{2,1,0:T(8,128)S(1)} %collective-permute-done.3.refs_1_, f32[2,64,128]{2,1,0:T(8,128)S(1)} %collective-permute-done.4.refs_2_, f32[2,64,128]{2,1,0:T(8,128)S(1)} %collective-permute-done.5.refs_3_, ...), custom_call_target="tpu_custom_call" | custom-call | tf_op jit(solution)/shard_map/column/pallas_call | solution.py:334
  (2 shorter events, 0.0 us)
Async XLA Ops:
  1.2 19.7 %collective-permute-start = (f32[7,8,512]{2,1,0:T(8,128)S(1)}, f32[7,8,512]{2,1,0:T(8,128)S(1)}, u32[]{:S(2)}, u32[]{:S(2)}) collective-permute-start(f32[7,8,512]{2,1,0:T(8,128)S(1)} %get-tuple-element.31), channel_id=1, source_target_pairs={{0,8},{8,0},{16,24},{24,16},{32,40},{40,32},{48,56},{56,48},{64,72... | collective-permute-start | bytes 344072 | tf_op jit(solution)/shard_map/ppermute | solution.py:265
  5.5 15.4 %collective-permute-start.1 = (f32[7,8,512]{2,1,0:T(8,128)S(1)}, f32[7,8,512]{2,1,0:T(8,128)S(1)}, u32[]{:S(2)}, u32[]{:S(2)}) collective-permute-start(f32[7,8,512]{2,1,0:T(8,128)S(1)} %get-tuple-element.32), channel_id=1, source_target_pairs={{8,16},{16,8},{24,32},{32,24},{40,48},{48,40},{56,64},{64,56},{72,... | collective-permute-start | bytes 344072 | tf_op jit(solution)/shard_map/ppermute | solution.py:265
  14.2 9.0 %collective-permute-start.6 = (f32[7,8,512]{2,1,0:T(8,128)S(1)}, f32[7,8,512]{2,1,0:T(8,128)S(1)}, u32[]{:S(2)}, u32[]{:S(2)}) collective-permute-start(f32[7,8,512]{2,1,0:T(8,128)S(1)} %get-tuple-element.39), channel_id=1, source_target_pairs={{0,8},{8,0},{16,24},{24,16},{32,40},{40,32},{48,56},{56,48},{64,72... | collective-permute-start | bytes 344072 | tf_op jit(solution)/shard_map/ppermute | solution.py:265
  16.1 4.1 %copy-start.2 = (f32[64]{0:T(128)S(1)}, f32[64]{0:T(128)}, u32[]{:S(2)}) copy-start(f32[64]{0:T(128)} %refs_2_.1) | copy-start | bytes 772
  16.2 4.1 %copy-start = (f32[2,64]{1,0:T(2,128)S(1)}, f32[2,64]{1,0:T(2,128)}, u32[]{:S(2)}) copy-start(f32[2,64]{1,0:T(2,128)} %refs_1_.1) | copy-start | bytes 1540
  16.2 4.1 %copy-start.1 = (s32[2,1]{0,1:T(1,128)S(1)}, s32[2,1]{0,1:T(1,128)}, u32[]{:S(2)}) copy-start(s32[2,1]{0,1:T(1,128)} %param.15) | copy-start | bytes 28
  16.2 11.6 %collective-permute-start.7 = (f32[7,8,512]{2,1,0:T(8,128)S(1)}, f32[7,8,512]{2,1,0:T(8,128)S(1)}, u32[]{:S(2)}, u32[]{:S(2)}) collective-permute-start(f32[7,8,512]{2,1,0:T(8,128)S(1)} %get-tuple-element.40), channel_id=1, source_target_pairs={{8,16},{16,8},{24,32},{32,24},{40,48},{48,40},{56,64},{64,56},{72,... | collective-permute-start | bytes 344072 | tf_op jit(solution)/shard_map/ppermute | solution.py:265
  21.3 8.8 %collective-permute-start.2 = (f32[2,64,128]{2,1,0:T(8,128)S(1)}, f32[2,64,128]{2,1,0:T(8,128)S(1)}, u32[]{:S(2)}, u32[]{:S(2)}) collective-permute-start(f32[2,64,128]{2,1,0:T(8,128)S(1)} %get-tuple-element.36), channel_id=1, source_target_pairs={{0,1},{1,0},{2,3},{3,2},{4,5},{5,4},{6,7},{7,6},{8,9},{9,8},{10,11... | collective-permute-start | bytes 196616 | tf_op jit(solution)/shard_map/ppermute | solution.py:270
  28.1 15.5 %collective-permute-start.8 = (f32[2,64,128]{2,1,0:T(8,128)S(1)}, f32[2,64,128]{2,1,0:T(8,128)S(1)}, u32[]{:S(2)}, u32[]{:S(2)}) collective-permute-start(f32[2,64,128]{2,1,0:T(8,128)S(1)} %get-tuple-element.42), channel_id=1, source_target_pairs={{0,1},{1,0},{2,3},{3,2},{4,5},{5,4},{6,7},{7,6},{8,9},{9,8},{10,11... | collective-permute-start | bytes 196616 | tf_op jit(solution)/shard_map/ppermute | solution.py:270
  30.1 21.8 %collective-permute-start.4 = (f32[2,64,128]{2,1,0:T(8,128)S(1)}, f32[2,64,128]{2,1,0:T(8,128)S(1)}, u32[]{:S(2)}, u32[]{:S(2)}) collective-permute-start(f32[2,64,128]{2,1,0:T(8,128)S(1)} %get-tuple-element.37.refs_0_), channel_id=1, source_target_pairs={{4,0},{5,1},{6,2},{7,3},{12,8},{13,9},{14,10},{15,11},{20,16},{21,... | collective-permute-start | bytes 196616 | tf_op jit(solution)/shard_map/ppermute | solution.py:274
  31.4 21.2 %collective-permute-start.5 = (f32[2,64,128]{2,1,0:T(8,128)S(1)}, f32[2,64,128]{2,1,0:T(8,128)S(1)}, u32[]{:S(2)}, u32[]{:S(2)}) collective-permute-start(f32[2,64,128]{2,1,0:T(8,128)S(1)} %get-tuple-element.38), channel_id=1, source_target_pairs={{4,2},{5,3},{6,0},{7,1},{12,10},{13,11},{14,8},{15,9},{20,18},{21,... | collective-permute-start | bytes 196616 | tf_op jit(solution)/shard_map/ppermute | solution.py:274
  32.7 19.9 %collective-permute-start.3 = (f32[2,64,128]{2,1,0:T(8,128)S(1)}, f32[2,64,128]{2,1,0:T(8,128)S(1)}, u32[]{:S(2)}, u32[]{:S(2)}) collective-permute-start(f32[2,64,128]{2,1,0:T(8,128)S(1)} %get-tuple-element.38), channel_id=1, source_target_pairs={{0,2},{1,3},{2,0},{3,1},{8,10},{9,11},{10,8},{11,9},{16,18},{17,19... | collective-permute-start | bytes 196616 | tf_op jit(solution)/shard_map/ppermute | solution.py:274
  43.6 9.4 %collective-permute-start.10 = (f32[2,64,128]{2,1,0:T(8,128)S(1)}, f32[2,64,128]{2,1,0:T(8,128)S(1)}, u32[]{:S(2)}, u32[]{:S(2)}) collective-permute-start(f32[2,64,128]{2,1,0:T(8,128)S(1)} %get-tuple-element.43.refs_4_), channel_id=1, source_target_pairs={{0,4},{1,5},{2,6},{3,7},{8,12},{9,13},{10,14},{11,15},{16,20},{17,... | collective-permute-start | bytes 196616 | tf_op jit(solution)/shard_map/ppermute | solution.py:274
  50.6 8.5 %collective-permute-start.11 = (f32[2,64,128]{2,1,0:T(8,128)S(1)}, f32[2,64,128]{2,1,0:T(8,128)S(1)}, u32[]{:S(2)}, u32[]{:S(2)}) collective-permute-start(f32[2,64,128]{2,1,0:T(8,128)S(1)} %get-tuple-element.44), channel_id=1, source_target_pairs={{0,6},{1,7},{2,4},{3,5},{8,14},{9,15},{10,12},{11,13},{16,22},{17,... | collective-permute-start | bytes 196616 | tf_op jit(solution)/shard_map/ppermute | solution.py:274
  51.9 7.2 %collective-permute-start.9 = (f32[2,64,128]{2,1,0:T(8,128)S(1)}, f32[2,64,128]{2,1,0:T(8,128)S(1)}, u32[]{:S(2)}, u32[]{:S(2)}) collective-permute-start(f32[2,64,128]{2,1,0:T(8,128)S(1)} %get-tuple-element.44), channel_id=1, source_target_pairs={{4,6},{5,7},{6,4},{7,5},{12,14},{13,15},{14,12},{15,13},{20,22},{2... | collective-permute-start | bytes 196616 | tf_op jit(solution)/shard_map/ppermute | solution.py:274

commit v5 on v3

--- a/solution.py
+++ b/solution.py
@@ -152,7 +152,7 @@
     return max(0, math.floor(low) - 1), min(levels, math.ceil(high) + 1)
 
 
-def column_body(sources, per, bands, own, beside, low2, high2, low3, high3, powers, daylight, out_h, got, thick_s, low_s, top_s, adv_s, pad_s, out, sems):
+def column_body(sources, per, bands, own, beside1, second1, third1, beside2, second2, third2, powers, daylight, out_h, got, low_s, top_s, pad_s, out, sems):
     levels = sources * per
     cols = LANES
     chip = lax.shift_right_logical(lax.axis_index("lev"), 1)
@@ -163,21 +163,31 @@
             for c in range(2):
                 got[2 * source + c] = piece[c]
 
-    pl.when(chip < 2)(lambda: place((own, beside, low2, low3)))
-    pl.when(chip >= 2)(lambda: place((own, beside, high2, high3)))
-    for r in range(2):
-        for s in range(sources):
-            for f in range(3):
-                adv_s[r, f, pl.ds(s * per, per), :] = got[s, pl.ds((r * 4 + f) * per, per), :]
-            thick_s[r, pl.ds(s * per, per), :] = got[s, pl.ds((r * 4 + 3) * per, per), :]
+    pl.when(chip < 2)(lambda: place((own, beside1, second1, third1)))
+    pl.when(chip >= 2)(lambda: place((own, beside2, second2, third2)))
     at_row = lax.broadcasted_iota(jnp.int32, (levels, levels), 0)
     at_col = lax.broadcasted_iota(jnp.int32, (levels, levels), 1)
-    triangle = jnp.where(at_row >= at_col, 1.0, 0.0).astype(jnp.float32)
+    triangle = jnp.where(at_row >= at_col, 1.0, 0.0).astype(jnp.bfloat16)
 
     def running(x):
-        return jnp.dot(triangle, x, precision=lax.Precision.HIGHEST, preferred_element_type=jnp.float32)
-
-    thick = jnp.concatenate([thick_s[0], thick_s[1]], axis=1)
+        total = None
+        for _ in range(3):
+            part = x.astype(jnp.bfloat16)
+            x = x - part.astype(jnp.float32)
+            sums = jnp.dot(triangle, part, preferred_element_type=jnp.float32)
+            total = sums if total is None else total + sums
+        return total
+
+    def piece(s, r, f):
+        return got[s, pl.ds((r * 4 + f) * per, per), :]
+
+    def level(j, r, f):
+        line = got[j // per, pl.ds((r * 4 + f) * per + j % per, 1), :]
+        return jnp.broadcast_to(line, (8, cols))
+
+    thick = jnp.concatenate(
+        [jnp.concatenate([piece(s, r, 3) for s in range(sources)], axis=0) for r in range(2)], axis=1
+    )
     top = running(thick)
     low = top - thick
     step = 8
@@ -203,7 +213,7 @@
                 edge_low = jnp.broadcast_to(low_s[r, pl.ds(j, 1), :], (step, cols))
                 shared = jnp.maximum(jnp.minimum(edge_top, ceiling) - jnp.maximum(edge_low, bottom), 0.0)
                 for f in range(3):
-                    sums[f] = sums[f] + shared * jnp.broadcast_to(adv_s[r, f, pl.ds(j, 1), :], (step, cols))
+                    sums[f] = sums[f] + shared * level(j, r, f)
             values = [total * inv8 for total in sums]
             pad_s[r, pl.ds(step + k, step), :] = values[0]
             out[1, pl.ds(2 * k + r, step, stride=2), :] = values[1]
@@ -308,30 +318,29 @@
         compiler_params=params,
         name="join",
     )(kept, core_swap(given_away))
-    beside = between_chips(beside, ((0, 1), (1, 0), (2, 3), (3, 2)))
-    low3 = between_chips(third, ((2, 1), (3, 0)))
-    low2 = between_chips(second, ((2, 0), (3, 1)))
-    high3 = between_chips(third, ((0, 3), (1, 2)))
-    high2 = between_chips(second, ((0, 2), (1, 3)))
+    third1 = between_chips(third, ((2, 1), (3, 0)))
+    second1 = between_chips(second, ((2, 0), (3, 1)))
+    beside1 = between_chips(beside, ((0, 1), (1, 0)))
+    third2 = between_chips(third, ((0, 3), (1, 2)))
+    second2 = between_chips(second, ((0, 2), (1, 3)))
+    beside2 = between_chips(beside, ((2, 3), (3, 2)))
     whole = sources * levels
     result = pl.pallas_call(
         lambda *refs: column_body(sources, levels, bands, *refs),
         out_shape=jax.ShapeDtypeStruct((3, whole * 2, LANES), jnp.float32),
-        in_specs=[vmem] * 8,
+        in_specs=[vmem] * 9,
         out_specs=hbm,
         scratch_shapes=[
             pltpu.VMEM((sources, 8 * levels, LANES), jnp.float32),
             pltpu.VMEM((2, whole, LANES), jnp.float32),
             pltpu.VMEM((2, whole, LANES), jnp.float32),
-            pltpu.VMEM((2, whole, LANES), jnp.float32),
-            pltpu.VMEM((2, 3, whole, LANES), jnp.float32),
             pltpu.VMEM((2, whole + 16, LANES), jnp.float32),
             pltpu.VMEM((3, whole * 2, LANES), jnp.float32),
             pltpu.SemaphoreType.DMA((3,)),
         ],
         compiler_params=params,
         name="column",
-    )(own, beside, low2, high2, low3, high3, powers, daylight)
+    )(own, beside1, second1, third1, beside2, second2, third2, powers, daylight)
     return result.reshape(3, whole, 2, LANES)
 
 

time: 73.9 us -> 74.3 us (level)
    ppermute x5 -> x6, starting transfers between devices: 35.2 us -> 35.9 us  [between_chips(): lax.ppermute(x, 'lev', [(2 * a + c, 2 * b + c) for a, b in pairs for c in...]
    ppermute x5 -> x6, waiting for transfers between devices: 8.8 us -> 8.8 us  [between_chips(): lax.ppermute(x, 'lev', [(2 * a + c, 2 * b + c) for a, b in pairs for c in...]
  transfers between devices with their start and end apart: 8 -> 9, of which waited for: 4 -> 4; matrix products, arithmetic and copies ran while one was open for 0% -> 0% of each run, Pallas kernels for 1% -> 1%
where the time goes in v5:
time: 74.3 us; the launch traced here: 74 us
  starting transfers between devices  50.9 us (69%)
  waiting for transfers between devices  17.9 us (24%)
  Pallas kernels  4.97 us (7%)
    ppermute x6, starting transfers between devices, between_chips(): lax.ppermute(x, 'lev', [(2 * a + c, 2 * b + c) for a, b in pairs for c in...  35.9 us
    ppermute x2, starting transfers between devices, swapped(): lax.ppermute(x, axis, [way for i, j in pairs for way in ((i, j), (j, i))])  13.1 us
    ppermute x6, waiting for transfers between devices, between_chips(): lax.ppermute(x, 'lev', [(2 * a + c, 2 * b + c) for a, b in pairs for c in...  8.8 us
    ppermute x2, waiting for transfers between devices, swapped(): lax.ppermute(x, axis, [way for i, j in pairs for way in ((i, j), (j, i))])  7.81 us
    pallas_call x1, Pallas kernels, local(): pl.pallas_call(lambda *refs: column_body(sources, levels, bands, *refs),...  2.69 us
    ppermute x1, starting transfers between devices, core_swap(): return lax.ppermute(x, 'lev', [(i, i ^ 1) for i in range(size)])  1.92 us
  transfers between devices with their start and end apart: 9, of which 4 were waited for; matrix products, arithmetic and copies ran while one was open for 0% of the time, Pallas kernels for 1%

profile of v5, /device:TPU:6, one launch (start us, length us, event | category | flops | bytes accessed | tf_op | source)
XLA Modules:
  0.0 74.0 jit_solution(16706065916348152214)
XLA Ops:
  0.0 1.2 %pack.1 = (f32[7,8,1024]{2,1,0:T(8,128)S(1)}, f32[7,8,1024]{2,1,0:T(8,128)S(1)}, f32[3,128,128]{2,1,0:T(8,128)S(1)}, f32[128,128]{1,0:T(8,128)S(1)}, f32[128,128...) custom-call(f32[3,128,128]{2,1,0:T(8,128)} %bitcast.33, ...), custom_call_target="tpu_custom_call" | custom-call | tf_op jit(solution)/shard_map/pack/pallas_call | solution.py:283
  1.2 4.3 %collective-permute-start = (f32[7,8,1024]{2,1,0:T(8,128)S(1)}, f32[7,8,1024]{2,1,0:T(8,128)S(1)}, u32[]{:S(2)}, u32[]{:S(2)}) collective-permute-start(f32[7,8,1024]{2,1,0:T(8,128)S(1)} %get-tuple-element.27), channel_id=1, source_target_pairs={{0,8},{8,0},{16,24},{24,16},{32,40},{40,32},{48,56},{56,48},{64,72... | collective-permute-start | bytes 688136 | tf_op jit(solution)/shard_map/ppermute | solution.py:260
  5.5 0.0 copy-start.2
  5.5 0.0 copy-start
  5.5 0.0 copy-start.1
  5.5 8.8 %collective-permute-start.1 = (f32[7,8,1024]{2,1,0:T(8,128)S(1)}, f32[7,8,1024]{2,1,0:T(8,128)S(1)}, u32[]{:S(2)}, u32[]{:S(2)}) collective-permute-start(f32[7,8,1024]{2,1,0:T(8,128)S(1)} %get-tuple-element.28), channel_id=1, source_target_pairs={{8,16},{16,8},{24,32},{32,24},{40,48},{48,40},{56,64},{64,56},{72,... | collective-permute-start | bytes 688136 | tf_op jit(solution)/shard_map/ppermute | solution.py:260
  14.4 0.0 copy-done.2
  14.4 0.0 copy-done
  14.4 0.0 copy-done.1
  14.4 0.7 prepare.1
  15.1 0.0 collective-permute-done.refs_6_
  15.1 7.8 %collective-permute-done.1.refs_7_ = f32[7,8,1024]{2,1,0:T(8,128)S(1)} collective-permute-done((f32[7,8,1024]{2,1,0:T(8,128)S(1)}, f32[7,8,1024]{2,1,0:T(8,128)S(1)}, u32[]{:S(2)}, u32[]{:S(2)}) %collective-permute-start.1) | collective-permute-done | bytes 229408 | tf_op jit(solution)/shard_map/ppermute | solution.py:260
  22.9 0.4 advect.1
  23.3 1.9 %collective-permute-start.2 = (f32[4,64,128]{2,1,0:T(8,128)S(1)}, f32[4,64,128]{2,1,0:T(8,128)S(1)}, u32[]{:S(2)}, u32[]{:S(2)}) collective-permute-start(f32[4,64,128]{2,1,0:T(8,128)S(1)} %get-tuple-element.32), channel_id=1, source_target_pairs={{0,1},{1,0},{2,3},{3,2},{4,5},{5,4},{6,7},{7,6},{8,9},{9,8},{10,11... | collective-permute-start | bytes 393224 | tf_op jit(solution)/shard_map/ppermute | solution.py:265
  25.2 1.3 %collective-permute-done.2.swapped_in = f32[4,64,128]{2,1,0:T(8,128)S(1)} collective-permute-done((f32[4,64,128]{2,1,0:T(8,128)S(1)}, f32[4,64,128]{2,1,0:T(8,128)S(1)}, u32[]{:S(2)}, u32[]{:S(2)}) %collective-permute-start.2) | collective-permute-done | bytes 131104 | tf_op jit(solution)/shard_map/ppermute | solution.py:265
  26.6 0.7 collective-permute-start.6
  27.2 10.9 %collective-permute-start.3 = (f32[2,64,128]{2,1,0:T(8,128)S(1)}, f32[2,64,128]{2,1,0:T(8,128)S(1)}, u32[]{:S(2)}, u32[]{:S(2)}) collective-permute-start(f32[2,64,128]{2,1,0:T(8,128)S(1)} %get-tuple-element.34), channel_id=1, source_target_pairs={{0,2},{1,3},{2,0},{3,1},{8,10},{9,11},{10,8},{11,9},{16,18},{17,19... | collective-permute-start | bytes 196616 | tf_op jit(solution)/shard_map/ppermute | solution.py:269
  38.2 12.1 %collective-permute-start.7 = (f32[2,64,128]{2,1,0:T(8,128)S(1)}, f32[2,64,128]{2,1,0:T(8,128)S(1)}, u32[]{:S(2)}, u32[]{:S(2)}) collective-permute-start(f32[2,64,128]{2,1,0:T(8,128)S(1)} %get-tuple-element.35), channel_id=1, source_target_pairs={{0,4},{1,5},{2,6},{3,7},{8,12},{9,13},{10,14},{11,15},{16,20},{17,... | collective-permute-start | bytes 196616 | tf_op jit(solution)/shard_map/ppermute | solution.py:269
  50.3 1.3 %collective-permute-start.4 = (f32[2,64,128]{2,1,0:T(8,128)S(1)}, f32[2,64,128]{2,1,0:T(8,128)S(1)}, u32[]{:S(2)}, u32[]{:S(2)}) collective-permute-start(f32[2,64,128]{2,1,0:T(8,128)S(1)} %get-tuple-element.35), channel_id=1, source_target_pairs={{4,0},{5,1},{6,2},{7,3},{12,8},{13,9},{14,10},{15,11},{20,16},{21,... | collective-permute-start | bytes 196616 | tf_op jit(solution)/shard_map/ppermute | solution.py:269
  51.6 9.6 %collective-permute-start.8 = (f32[2,64,128]{2,1,0:T(8,128)S(1)}, f32[2,64,128]{2,1,0:T(8,128)S(1)}, u32[]{:S(2)}, u32[]{:S(2)}) collective-permute-start(f32[2,64,128]{2,1,0:T(8,128)S(1)} %get-tuple-element.36), channel_id=1, source_target_pairs={{0,6},{1,7},{2,4},{3,5},{8,14},{9,15},{10,12},{11,13},{16,22},{17,... | collective-permute-start | bytes 196616 | tf_op jit(solution)/shard_map/ppermute | solution.py:269
  61.2 0.0 collective-permute-done.6.refs_4_
  61.2 1.3 %collective-permute-start.5 = (f32[2,64,128]{2,1,0:T(8,128)S(1)}, f32[2,64,128]{2,1,0:T(8,128)S(1)}, u32[]{:S(2)}, u32[]{:S(2)}) collective-permute-start(f32[2,64,128]{2,1,0:T(8,128)S(1)} %get-tuple-element.36), channel_id=1, source_target_pairs={{4,2},{5,3},{6,0},{7,1},{12,10},{13,11},{14,8},{15,9},{20,18},{21,... | collective-permute-start | bytes 196616 | tf_op jit(solution)/shard_map/ppermute | solution.py:269
  62.5 0.0 collective-permute-done.3.refs_1_
  62.5 0.0 collective-permute-done.7.refs_5_
  62.6 2.7 %collective-permute-done.4.refs_2_ = f32[2,64,128]{2,1,0:T(8,128)S(1)} collective-permute-done((f32[2,64,128]{2,1,0:T(8,128)S(1)}, f32[2,64,128]{2,1,0:T(8,128)S(1)}, u32[]{:S(2)}, u32[]{:S(2)}) %collective-permute-start.4) | collective-permute-done | bytes 65568 | tf_op jit(solution)/shard_map/ppermute | solution.py:269
  65.2 0.0 collective-permute-done.8.refs_6_
  65.2 6.1 %collective-permute-done.5.refs_3_ = f32[2,64,128]{2,1,0:T(8,128)S(1)} collective-permute-done((f32[2,64,128]{2,1,0:T(8,128)S(1)}, f32[2,64,128]{2,1,0:T(8,128)S(1)}, u32[]{:S(2)}, u32[]{:S(2)}) %collective-permute-start.5) | collective-permute-done | bytes 65568 | tf_op jit(solution)/shard_map/ppermute | solution.py:269
  71.4 2.7 %column.1 = f32[3,128,128]{2,1,0:T(8,128)} custom-call(f32[2,64,128]{2,1,0:T(8,128)S(1)} %get-tuple-element.33.refs_0_, f32[2,64,128]{2,1,0:T(8,128)S(1)} %collective-permute-done.3.refs_1_, f32[2,64,128]{2,1,0:T(8,128)S(1)} %collective-permute-done.4.refs_2_, f32[2,64,128]{2,1,0:T(8,128)S(1)} %collective-permute-done.5.refs_3_, ...), custom_call_target="tpu_custom_call" | custom-call | tf_op jit(solution)/shard_map/column/pallas_call | solution.py:328
  (1 shorter events, 0.0 us)
Async XLA Ops:
  1.2 13.9 %collective-permute-start = (f32[7,8,1024]{2,1,0:T(8,128)S(1)}, f32[7,8,1024]{2,1,0:T(8,128)S(1)}, u32[]{:S(2)}, u32[]{:S(2)}) collective-permute-start(f32[7,8,1024]{2,1,0:T(8,128)S(1)} %get-tuple-element.27), channel_id=1, source_target_pairs={{0,8},{8,0},{16,24},{24,16},{32,40},{40,32},{48,56},{56,48},{64,72... | collective-permute-start | bytes 688136 | tf_op jit(solution)/shard_map/ppermute | solution.py:260
  5.5 8.9 %copy-start.2 = (f32[64]{0:T(128)S(1)}, f32[64]{0:T(128)}, u32[]{:S(2)}) copy-start(f32[64]{0:T(128)} %refs_2_.1) | copy-start | bytes 772
  5.5 8.9 %copy-start = (f32[2,64]{1,0:T(2,128)S(1)}, f32[2,64]{1,0:T(2,128)}, u32[]{:S(2)}) copy-start(f32[2,64]{1,0:T(2,128)} %refs_1_.1) | copy-start | bytes 1540
  5.5 8.9 %copy-start.1 = (s32[2,1]{0,1:T(1,128)S(1)}, s32[2,1]{0,1:T(1,128)}, u32[]{:S(2)}) copy-start(s32[2,1]{0,1:T(1,128)} %param.15) | copy-start | bytes 28
  5.5 17.4 %collective-permute-start.1 = (f32[7,8,1024]{2,1,0:T(8,128)S(1)}, f32[7,8,1024]{2,1,0:T(8,128)S(1)}, u32[]{:S(2)}, u32[]{:S(2)}) collective-permute-start(f32[7,8,1024]{2,1,0:T(8,128)S(1)} %get-tuple-element.28), channel_id=1, source_target_pairs={{8,16},{16,8},{24,32},{32,24},{40,48},{48,40},{56,64},{64,56},{72,... | collective-permute-start | bytes 688136 | tf_op jit(solution)/shard_map/ppermute | solution.py:260
  23.3 3.2 %collective-permute-start.2 = (f32[4,64,128]{2,1,0:T(8,128)S(1)}, f32[4,64,128]{2,1,0:T(8,128)S(1)}, u32[]{:S(2)}, u32[]{:S(2)}) collective-permute-start(f32[4,64,128]{2,1,0:T(8,128)S(1)} %get-tuple-element.32), channel_id=1, source_target_pairs={{0,1},{1,0},{2,3},{3,2},{4,5},{5,4},{6,7},{7,6},{8,9},{9,8},{10,11... | collective-permute-start | bytes 393224 | tf_op jit(solution)/shard_map/ppermute | solution.py:265
  26.6 34.7 %collective-permute-start.6 = (f32[2,64,128]{2,1,0:T(8,128)S(1)}, f32[2,64,128]{2,1,0:T(8,128)S(1)}, u32[]{:S(2)}, u32[]{:S(2)}) collective-permute-start(f32[2,64,128]{2,1,0:T(8,128)S(1)} %get-tuple-element.34), channel_id=1, source_target_pairs={{4,6},{5,7},{6,4},{7,5},{12,14},{13,15},{14,12},{15,13},{20,22},{2... | collective-permute-start | bytes 196616 | tf_op jit(solution)/shard_map/ppermute | solution.py:269
  27.2 35.3 %collective-permute-start.3 = (f32[2,64,128]{2,1,0:T(8,128)S(1)}, f32[2,64,128]{2,1,0:T(8,128)S(1)}, u32[]{:S(2)}, u32[]{:S(2)}) collective-permute-start(f32[2,64,128]{2,1,0:T(8,128)S(1)} %get-tuple-element.34), channel_id=1, source_target_pairs={{0,2},{1,3},{2,0},{3,1},{8,10},{9,11},{10,8},{11,9},{16,18},{17,19... | collective-permute-start | bytes 196616 | tf_op jit(solution)/shard_map/ppermute | solution.py:269
  38.2 24.4 %collective-permute-start.7 = (f32[2,64,128]{2,1,0:T(8,128)S(1)}, f32[2,64,128]{2,1,0:T(8,128)S(1)}, u32[]{:S(2)}, u32[]{:S(2)}) collective-permute-start(f32[2,64,128]{2,1,0:T(8,128)S(1)} %get-tuple-element.35), channel_id=1, source_target_pairs={{0,4},{1,5},{2,6},{3,7},{8,12},{9,13},{10,14},{11,15},{16,20},{17,... | collective-permute-start | bytes 196616 | tf_op jit(solution)/shard_map/ppermute | solution.py:269
  50.3 14.9 %collective-permute-start.4 = (f32[2,64,128]{2,1,0:T(8,128)S(1)}, f32[2,64,128]{2,1,0:T(8,128)S(1)}, u32[]{:S(2)}, u32[]{:S(2)}) collective-permute-start(f32[2,64,128]{2,1,0:T(8,128)S(1)} %get-tuple-element.35), channel_id=1, source_target_pairs={{4,0},{5,1},{6,2},{7,3},{12,8},{13,9},{14,10},{15,11},{20,16},{21,... | collective-permute-start | bytes 196616 | tf_op jit(solution)/shard_map/ppermute | solution.py:269
  51.6 13.6 %collective-permute-start.8 = (f32[2,64,128]{2,1,0:T(8,128)S(1)}, f32[2,64,128]{2,1,0:T(8,128)S(1)}, u32[]{:S(2)}, u32[]{:S(2)}) collective-permute-start(f32[2,64,128]{2,1,0:T(8,128)S(1)} %get-tuple-element.36), channel_id=1, source_target_pairs={{0,6},{1,7},{2,4},{3,5},{8,14},{9,15},{10,12},{11,13},{16,22},{17,... | collective-permute-start | bytes 196616 | tf_op jit(solution)/shard_map/ppermute | solution.py:269
  61.2 10.1 %collective-permute-start.5 = (f32[2,64,128]{2,1,0:T(8,128)S(1)}, f32[2,64,128]{2,1,0:T(8,128)S(1)}, u32[]{:S(2)}, u32[]{:S(2)}) collective-permute-start(f32[2,64,128]{2,1,0:T(8,128)S(1)} %get-tuple-element.36), channel_id=1, source_target_pairs={{4,2},{5,3},{6,0},{7,1},{12,10},{13,11},{14,8},{15,9},{20,18},{21,... | collective-permute-start | bytes 196616 | tf_op jit(solution)/shard_map/ppermute | solution.py:269

commit v6 on v5

--- a/solution.py
+++ b/solution.py
@@ -152,19 +152,18 @@
     return max(0, math.floor(low) - 1), min(levels, math.ceil(high) + 1)
 
 
-def column_body(sources, per, bands, own, beside1, second1, third1, beside2, second2, third2, powers, daylight, out_h, got, low_s, top_s, pad_s, out, sems):
+def column_body(upper, *refs):
+    chip = lax.shift_right_logical(lax.axis_index("lev"), 1)
+    pl.when((chip >= 2) if upper else (chip < 2))(lambda: columns(chip, *refs))
+
+
+def columns(chip, sources, per, bands, own, beside, second, third, powers, daylight, out_h, got, low_s, top_s, pad_s, out, sems):
     levels = sources * per
     cols = LANES
-    chip = lax.shift_right_logical(lax.axis_index("lev"), 1)
-
-    def place(pieces):
-        for q, piece in enumerate(pieces):
-            source = lax.bitwise_xor(chip, q)
-            for c in range(2):
-                got[2 * source + c] = piece[c]
-
-    pl.when(chip < 2)(lambda: place((own, beside1, second1, third1)))
-    pl.when(chip >= 2)(lambda: place((own, beside2, second2, third2)))
+    for q, piece in enumerate((own, beside, second, third)):
+        source = lax.bitwise_xor(chip, q)
+        for c in range(2):
+            got[2 * source + c] = piece[c]
     at_row = lax.broadcasted_iota(jnp.int32, (levels, levels), 0)
     at_col = lax.broadcasted_iota(jnp.int32, (levels, levels), 1)
     triangle = jnp.where(at_row >= at_col, 1.0, 0.0).astype(jnp.bfloat16)
@@ -178,7 +177,7 @@
             total = sums if total is None else total + sums
         return total
 
-    def piece(s, r, f):
+    def part_of(s, r, f):
         return got[s, pl.ds((r * 4 + f) * per, per), :]
 
     def level(j, r, f):
@@ -186,7 +185,7 @@
         return jnp.broadcast_to(line, (8, cols))
 
     thick = jnp.concatenate(
-        [jnp.concatenate([piece(s, r, 3) for s in range(sources)], axis=0) for r in range(2)], axis=1
+        [jnp.concatenate([part_of(s, r, 3) for s in range(sources)], axis=0) for r in range(2)], axis=1
     )
     top = running(thick)
     low = top - thick
@@ -325,22 +324,34 @@
     second2 = between_chips(second, ((0, 2), (1, 3)))
     beside2 = between_chips(beside, ((2, 3), (3, 2)))
     whole = sources * levels
+    shape = jax.ShapeDtypeStruct((3, whole * 2, LANES), jnp.float32)
+    scratch = [
+        pltpu.VMEM((sources, 8 * levels, LANES), jnp.float32),
+        pltpu.VMEM((2, whole, LANES), jnp.float32),
+        pltpu.VMEM((2, whole, LANES), jnp.float32),
+        pltpu.VMEM((2, whole + 16, LANES), jnp.float32),
+        pltpu.VMEM((3, whole * 2, LANES), jnp.float32),
+        pltpu.SemaphoreType.DMA((3,)),
+    ]
     result = pl.pallas_call(
-        lambda *refs: column_body(sources, levels, bands, *refs),
-        out_shape=jax.ShapeDtypeStruct((3, whole * 2, LANES), jnp.float32),
-        in_specs=[vmem] * 9,
+        lambda *refs: column_body(False, sources, levels, bands, *refs),
+        out_shape=shape,
+        in_specs=[vmem] * 6,
         out_specs=hbm,
-        scratch_shapes=[
-            pltpu.VMEM((sources, 8 * levels, LANES), jnp.float32),
-            pltpu.VMEM((2, whole, LANES), jnp.float32),
-            pltpu.VMEM((2, whole, LANES), jnp.float32),
-            pltpu.VMEM((2, whole + 16, LANES), jnp.float32),
-            pltpu.VMEM((3, whole * 2, LANES), jnp.float32),
-            pltpu.SemaphoreType.DMA((3,)),
-        ],
-        compiler_params=params,
-        name="column",
-    )(own, beside1, second1, third1, beside2, second2, third2, powers, daylight)
+        scratch_shapes=scratch,
+        compiler_params=params,
+        name="column_lower",
+    )(own, beside1, second1, third1, powers, daylight)
+    result = pl.pallas_call(
+        lambda *refs: column_body(True, sources, levels, bands, *refs[1:]),
+        out_shape=shape,
+        in_specs=[hbm] + [vmem] * 6,
+        out_specs=hbm,
+        input_output_aliases={0: 0},
+        scratch_shapes=scratch,
+        compiler_params=params,
+        name="column_upper",
+    )(result, own, beside2, second2, third2, powers, daylight)
     return result.reshape(3, whole, 2, LANES)
 
 

time: 74.3 us -> 65.8 us (0.89)
  starting transfers between devices: 50.9 us -> 45.6 us
  waiting for transfers between devices: 17.9 us -> 14.6 us
    ppermute x6, starting transfers between devices: 35.9 us -> 30.5 us  [between_chips(): lax.ppermute(x, 'lev', [(2 * a + c, 2 * b + c) for a, b in pairs for c in...]
    ppermute x6, waiting for transfers between devices: 8.8 us -> 5.48 us  [between_chips(): lax.ppermute(x, 'lev', [(2 * a + c, 2 * b + c) for a, b in pairs for c in...]
    pallas_call x1 -> x2, Pallas kernels: 2.69 us -> 2.71 us  [the longest x1 2.69 us: local(): pl.pallas_call(lambda *refs: column_body(False, sources, levels, bands, *...]
  transfers between devices with their start and end apart: 9 -> 9, of which waited for: 4 -> 3; matrix products, arithmetic and copies ran while one was open for 0% -> 0% of each run, Pallas kernels for 1% -> 5%
where the time goes in v6:
time: 65.8 us; the launch traced here: 65.4 us
  starting transfers between devices  45.6 us (69%)
  waiting for transfers between devices  14.6 us (22%)
  Pallas kernels  5 us (8%)
    ppermute x6, starting transfers between devices, between_chips(): lax.ppermute(x, 'lev', [(2 * a + c, 2 * b + c) for a, b in pairs for c in...  30.5 us
    ppermute x2, starting transfers between devices, swapped(): lax.ppermute(x, axis, [way for i, j in pairs for way in ((i, j), (j, i))])  13.1 us
    ppermute x2, waiting for transfers between devices, swapped(): lax.ppermute(x, axis, [way for i, j in pairs for way in ((i, j), (j, i))])  7.81 us
    ppermute x6, waiting for transfers between devices, between_chips(): lax.ppermute(x, 'lev', [(2 * a + c, 2 * b + c) for a, b in pairs for c in...  5.48 us
    pallas_call x1, Pallas kernels, local(): pl.pallas_call(lambda *refs: column_body(False, sources, levels, bands, *...  2.69 us
    ppermute x1, starting transfers between devices, core_swap(): return lax.ppermute(x, 'lev', [(i, i ^ 1) for i in range(size)])  1.92 us
  transfers between devices with their start and end apart: 9, of which 3 were waited for; matrix products, arithmetic and copies ran while one was open for 0% of the time, Pallas kernels for 5%

profile of v6, /device:TPU:6, one launch (start us, length us, event | category | flops | bytes accessed | tf_op | source)
XLA Modules:
  0.0 65.4 jit_solution(17038753413230386334)
XLA Ops:
  0.0 1.2 %pack.1 = (f32[7,8,1024]{2,1,0:T(8,128)S(1)}, f32[7,8,1024]{2,1,0:T(8,128)S(1)}, f32[3,128,128]{2,1,0:T(8,128)S(1)}, f32[128,128]{1,0:T(8,128)S(1)}, f32[128,128...) custom-call(f32[3,128,128]{2,1,0:T(8,128)} %bitcast.33, ...), custom_call_target="tpu_custom_call" | custom-call | tf_op jit(solution)/shard_map/pack/pallas_call | solution.py:282
  1.2 4.3 %collective-permute-start = (f32[7,8,1024]{2,1,0:T(8,128)S(1)}, f32[7,8,1024]{2,1,0:T(8,128)S(1)}, u32[]{:S(2)}, u32[]{:S(2)}) collective-permute-start(f32[7,8,1024]{2,1,0:T(8,128)S(1)} %get-tuple-element.27), channel_id=1, source_target_pairs={{0,8},{8,0},{16,24},{24,16},{32,40},{40,32},{48,56},{56,48},{64,72... | collective-permute-start | bytes 688136 | tf_op jit(solution)/shard_map/ppermute | solution.py:259
  5.5 0.0 copy-start.2
  5.5 0.0 copy-start
  5.5 0.0 copy-start.1
  5.5 8.8 %collective-permute-start.1 = (f32[7,8,1024]{2,1,0:T(8,128)S(1)}, f32[7,8,1024]{2,1,0:T(8,128)S(1)}, u32[]{:S(2)}, u32[]{:S(2)}) collective-permute-start(f32[7,8,1024]{2,1,0:T(8,128)S(1)} %get-tuple-element.28), channel_id=1, source_target_pairs={{8,16},{16,8},{24,32},{32,24},{40,48},{48,40},{56,64},{64,56},{72,... | collective-permute-start | bytes 688136 | tf_op jit(solution)/shard_map/ppermute | solution.py:259
  14.4 0.0 copy-done.2
  14.4 0.0 copy-done
  14.4 0.0 copy-done.1
  14.4 0.7 prepare.1
  15.1 0.0 collective-permute-done.refs_6_
  15.1 7.8 %collective-permute-done.1.refs_7_ = f32[7,8,1024]{2,1,0:T(8,128)S(1)} collective-permute-done((f32[7,8,1024]{2,1,0:T(8,128)S(1)}, f32[7,8,1024]{2,1,0:T(8,128)S(1)}, u32[]{:S(2)}, u32[]{:S(2)}) %collective-permute-start.1) | collective-permute-done | bytes 229408 | tf_op jit(solution)/shard_map/ppermute | solution.py:259
  22.9 0.4 advect.1
  23.3 1.9 %collective-permute-start.2 = (f32[4,64,128]{2,1,0:T(8,128)S(1)}, f32[4,64,128]{2,1,0:T(8,128)S(1)}, u32[]{:S(2)}, u32[]{:S(2)}) collective-permute-start(f32[4,64,128]{2,1,0:T(8,128)S(1)} %get-tuple-element.32), channel_id=1, source_target_pairs={{0,1},{1,0},{2,3},{3,2},{4,5},{5,4},{6,7},{7,6},{8,9},{9,8},{10,11... | collective-permute-start | bytes 393224 | tf_op jit(solution)/shard_map/ppermute | solution.py:264
  25.2 1.3 %collective-permute-done.2.swapped_in = f32[4,64,128]{2,1,0:T(8,128)S(1)} collective-permute-done((f32[4,64,128]{2,1,0:T(8,128)S(1)}, f32[4,64,128]{2,1,0:T(8,128)S(1)}, u32[]{:S(2)}, u32[]{:S(2)}) %collective-permute-start.2) | collective-permute-done | bytes 131104 | tf_op jit(solution)/shard_map/ppermute | solution.py:264
  26.6 10.9 %collective-permute-start.3 = (f32[2,64,128]{2,1,0:T(8,128)S(1)}, f32[2,64,128]{2,1,0:T(8,128)S(1)}, u32[]{:S(2)}, u32[]{:S(2)}) collective-permute-start(f32[2,64,128]{2,1,0:T(8,128)S(1)} %get-tuple-element.34), channel_id=1, source_target_pairs={{0,2},{1,3},{2,0},{3,1},{8,10},{9,11},{10,8},{11,9},{16,18},{17,19... | collective-permute-start | bytes 196616 | tf_op jit(solution)/shard_map/ppermute | solution.py:268
  37.5 1.3 %collective-permute-start.4 = (f32[2,64,128]{2,1,0:T(8,128)S(1)}, f32[2,64,128]{2,1,0:T(8,128)S(1)}, u32[]{:S(2)}, u32[]{:S(2)}) collective-permute-start(f32[2,64,128]{2,1,0:T(8,128)S(1)} %get-tuple-element.35), channel_id=1, source_target_pairs={{4,0},{5,1},{6,2},{7,3},{12,8},{13,9},{14,10},{15,11},{20,16},{21,... | collective-permute-start | bytes 196616 | tf_op jit(solution)/shard_map/ppermute | solution.py:268
  38.8 1.3 %collective-permute-start.5 = (f32[2,64,128]{2,1,0:T(8,128)S(1)}, f32[2,64,128]{2,1,0:T(8,128)S(1)}, u32[]{:S(2)}, u32[]{:S(2)}) collective-permute-start(f32[2,64,128]{2,1,0:T(8,128)S(1)} %get-tuple-element.36), channel_id=1, source_target_pairs={{4,2},{5,3},{6,0},{7,1},{12,10},{13,11},{14,8},{15,9},{20,18},{21,... | collective-permute-start | bytes 196616 | tf_op jit(solution)/shard_map/ppermute | solution.py:268
  40.1 0.7 %collective-permute-start.6 = (f32[2,64,128]{2,1,0:T(8,128)S(1)}, f32[2,64,128]{2,1,0:T(8,128)S(1)}, u32[]{:S(2)}, u32[]{:S(2)}) collective-permute-start(f32[2,64,128]{2,1,0:T(8,128)S(1)} %get-tuple-element.34), channel_id=1, source_target_pairs={{4,6},{5,7},{6,4},{7,5},{12,14},{13,15},{14,12},{15,13},{20,22},{2... | collective-permute-start | bytes 196616 | tf_op jit(solution)/shard_map/ppermute | solution.py:268
  40.8 15.1 %collective-permute-start.7 = (f32[2,64,128]{2,1,0:T(8,128)S(1)}, f32[2,64,128]{2,1,0:T(8,128)S(1)}, u32[]{:S(2)}, u32[]{:S(2)}) collective-permute-start(f32[2,64,128]{2,1,0:T(8,128)S(1)} %get-tuple-element.35), channel_id=1, source_target_pairs={{0,4},{1,5},{2,6},{3,7},{8,12},{9,13},{10,14},{11,15},{16,20},{17,... | collective-permute-start | bytes 196616 | tf_op jit(solution)/shard_map/ppermute | solution.py:268
  55.8 0.0 collective-permute-done.3.refs_1_
  55.9 1.3 %collective-permute-start.8 = (f32[2,64,128]{2,1,0:T(8,128)S(1)}, f32[2,64,128]{2,1,0:T(8,128)S(1)}, u32[]{:S(2)}, u32[]{:S(2)}) collective-permute-start(f32[2,64,128]{2,1,0:T(8,128)S(1)} %get-tuple-element.36), channel_id=1, source_target_pairs={{0,6},{1,7},{2,4},{3,5},{8,14},{9,15},{10,12},{11,13},{16,22},{17,... | collective-permute-start | bytes 196616 | tf_op jit(solution)/shard_map/ppermute | solution.py:268
  57.2 0.0 collective-permute-done.4.refs_2_
  57.2 0.0 collective-permute-done.5.refs_3_
  57.2 2.7 %column_lower.1.refs_0_ = f32[3,128,128]{2,1,0:T(8,128)} custom-call(f32[2,64,128]{2,1,0:T(8,128)S(1)} %get-tuple-element.33.refs_0_.refs_1_, f32[2,64,128]{2,1,0:T(8,128)S(1)} %collective-permute-done.3.refs_1_, f32[2,64,128]{2,1,0:T(8,128)S(1)} %collective-permute-done.4.refs_2_, f32[2,64,128]{2,1,0:T(8,128)S(1)} %collective-permute-done.5.refs_3_, ...), custom_call_target="tpu_custom_call" | custom-call | tf_op jit(solution)/shard_map/column_lower/pallas_call | solution.py:336
  59.9 0.0 collective-permute-done.6.refs_2_
  59.9 0.0 collective-permute-done.7.refs_3_
  59.9 5.5 %collective-permute-done.8.refs_4_ = f32[2,64,128]{2,1,0:T(8,128)S(1)} collective-permute-done((f32[2,64,128]{2,1,0:T(8,128)S(1)}, f32[2,64,128]{2,1,0:T(8,128)S(1)}, u32[]{:S(2)}, u32[]{:S(2)}) %collective-permute-start.8) | collective-permute-done | bytes 65568 | tf_op jit(solution)/shard_map/ppermute | solution.py:268
  (2 shorter events, 0.0 us)
Async XLA Ops:
  1.2 13.9 %collective-permute-start = (f32[7,8,1024]{2,1,0:T(8,128)S(1)}, f32[7,8,1024]{2,1,0:T(8,128)S(1)}, u32[]{:S(2)}, u32[]{:S(2)}) collective-permute-start(f32[7,8,1024]{2,1,0:T(8,128)S(1)} %get-tuple-element.27), channel_id=1, source_target_pairs={{0,8},{8,0},{16,24},{24,16},{32,40},{40,32},{48,56},{56,48},{64,72... | collective-permute-start | bytes 688136 | tf_op jit(solution)/shard_map/ppermute | solution.py:259
  5.5 8.9 %copy-start.2 = (f32[64]{0:T(128)S(1)}, f32[64]{0:T(128)}, u32[]{:S(2)}) copy-start(f32[64]{0:T(128)} %refs_2_.1) | copy-start | bytes 772
  5.5 8.9 %copy-start = (f32[2,64]{1,0:T(2,128)S(1)}, f32[2,64]{1,0:T(2,128)}, u32[]{:S(2)}) copy-start(f32[2,64]{1,0:T(2,128)} %refs_1_.1) | copy-start | bytes 1540
  5.5 8.9 %copy-start.1 = (s32[2,1]{0,1:T(1,128)S(1)}, s32[2,1]{0,1:T(1,128)}, u32[]{:S(2)}) copy-start(s32[2,1]{0,1:T(1,128)} %param.15) | copy-start | bytes 28
  5.5 17.4 %collective-permute-start.1 = (f32[7,8,1024]{2,1,0:T(8,128)S(1)}, f32[7,8,1024]{2,1,0:T(8,128)S(1)}, u32[]{:S(2)}, u32[]{:S(2)}) collective-permute-start(f32[7,8,1024]{2,1,0:T(8,128)S(1)} %get-tuple-element.28), channel_id=1, source_target_pairs={{8,16},{16,8},{24,32},{32,24},{40,48},{48,40},{56,64},{64,56},{72,... | collective-permute-start | bytes 688136 | tf_op jit(solution)/shard_map/ppermute | solution.py:259
  23.3 3.2 %collective-permute-start.2 = (f32[4,64,128]{2,1,0:T(8,128)S(1)}, f32[4,64,128]{2,1,0:T(8,128)S(1)}, u32[]{:S(2)}, u32[]{:S(2)}) collective-permute-start(f32[4,64,128]{2,1,0:T(8,128)S(1)} %get-tuple-element.32), channel_id=1, source_target_pairs={{0,1},{1,0},{2,3},{3,2},{4,5},{5,4},{6,7},{7,6},{8,9},{9,8},{10,11... | collective-permute-start | bytes 393224 | tf_op jit(solution)/shard_map/ppermute | solution.py:264
  26.6 29.3 %collective-permute-start.3 = (f32[2,64,128]{2,1,0:T(8,128)S(1)}, f32[2,64,128]{2,1,0:T(8,128)S(1)}, u32[]{:S(2)}, u32[]{:S(2)}) collective-permute-start(f32[2,64,128]{2,1,0:T(8,128)S(1)} %get-tuple-element.34), channel_id=1, source_target_pairs={{0,2},{1,3},{2,0},{3,1},{8,10},{9,11},{10,8},{11,9},{16,18},{17,19... | collective-permute-start | bytes 196616 | tf_op jit(solution)/shard_map/ppermute | solution.py:268
  37.5 19.7 %collective-permute-start.4 = (f32[2,64,128]{2,1,0:T(8,128)S(1)}, f32[2,64,128]{2,1,0:T(8,128)S(1)}, u32[]{:S(2)}, u32[]{:S(2)}) collective-permute-start(f32[2,64,128]{2,1,0:T(8,128)S(1)} %get-tuple-element.35), channel_id=1, source_target_pairs={{4,0},{5,1},{6,2},{7,3},{12,8},{13,9},{14,10},{15,11},{20,16},{21,... | collective-permute-start | bytes 196616 | tf_op jit(solution)/shard_map/ppermute | solution.py:268
  38.8 18.4 %collective-permute-start.5 = (f32[2,64,128]{2,1,0:T(8,128)S(1)}, f32[2,64,128]{2,1,0:T(8,128)S(1)}, u32[]{:S(2)}, u32[]{:S(2)}) collective-permute-start(f32[2,64,128]{2,1,0:T(8,128)S(1)} %get-tuple-element.36), channel_id=1, source_target_pairs={{4,2},{5,3},{6,0},{7,1},{12,10},{13,11},{14,8},{15,9},{20,18},{21,... | collective-permute-start | bytes 196616 | tf_op jit(solution)/shard_map/ppermute | solution.py:268
  40.1 19.8 %collective-permute-start.6 = (f32[2,64,128]{2,1,0:T(8,128)S(1)}, f32[2,64,128]{2,1,0:T(8,128)S(1)}, u32[]{:S(2)}, u32[]{:S(2)}) collective-permute-start(f32[2,64,128]{2,1,0:T(8,128)S(1)} %get-tuple-element.34), channel_id=1, source_target_pairs={{4,6},{5,7},{6,4},{7,5},{12,14},{13,15},{14,12},{15,13},{20,22},{2... | collective-permute-start | bytes 196616 | tf_op jit(solution)/shard_map/ppermute | solution.py:268
  40.8 19.1 %collective-permute-start.7 = (f32[2,64,128]{2,1,0:T(8,128)S(1)}, f32[2,64,128]{2,1,0:T(8,128)S(1)}, u32[]{:S(2)}, u32[]{:S(2)}) collective-permute-start(f32[2,64,128]{2,1,0:T(8,128)S(1)} %get-tuple-element.35), channel_id=1, source_target_pairs={{0,4},{1,5},{2,6},{3,7},{8,12},{9,13},{10,14},{11,15},{16,20},{17,... | collective-permute-start | bytes 196616 | tf_op jit(solution)/shard_map/ppermute | solution.py:268
  55.9 9.5 %collective-permute-start.8 = (f32[2,64,128]{2,1,0:T(8,128)S(1)}, f32[2,64,128]{2,1,0:T(8,128)S(1)}, u32[]{:S(2)}, u32[]{:S(2)}) collective-permute-start(f32[2,64,128]{2,1,0:T(8,128)S(1)} %get-tuple-element.36), channel_id=1, source_target_pairs={{0,6},{1,7},{2,4},{3,5},{8,14},{9,15},{10,12},{11,13},{16,22},{17,... | collective-permute-start | bytes 196616 | tf_op jit(solution)/shard_map/ppermute | solution.py:268
